TPU v7x, 32 devices: a whole 2x2x4 slice. The times are simulated.
32 devices in a mesh: lm: 8 (over z, x), kf: 4 (over y, core).
Axes of the slice: x: 2, y: 2, z: 4, core: 2. Of those that a mesh axis runs over, the one named last changes fastest.
Arguments:
- residual_rows: bfloat16 [4096, 128], P(('lm', 'kf')), may hold values from -6 to 6
- jacobian: bfloat16 [4096, 15, 128], P(('lm', 'kf')), may hold values from -1.5 to 1.5
- nullspace: bfloat16 [4096, 128, 128], P(('lm', 'kf')), may hold values from -0.5 to 0.5
- frame_ids: int32 [4096, 64], P(('lm', 'kf')), may hold values from 0 to 16383, as said below
- obs_count: int32 [4096], P(('lm', 'kf')), may hold values from 4 to 64
- damping: float32 [15, 16384], P(None, 'kf'), may hold values from 1 to 10
- jacobi_scale: float32 [15, 16384], P(None, 'kf'), may hold values from 0.02 to 0.3
Outputs:
- solution: float32 [15, 16384], P(None, 'kf')
- residual: float32 [15, 16384], P(None, 'kf')
Inputs may be any that keep to these rules, and one draw needn't show every extreme that they name: `frame_ids`: within a block the keyframe ids rise strictly from slot to slot by 1 to 8. A block stored on the device with kf index w names only keyframes from 4096 * w up to but not including 4096 * (w + 2), and never one of 16384 or more.
All inputs are finite; a program needn't handle non-finite values.
Results may differ from a plain program's by a relative error of at most 0.005.
Values sent between devices are 32-bit elements; how exact they have to be, the bound alone decides.
A program may use at most 64 MiB of HBM per device.

v0:
```python
import functools

import jax
import jax.numpy as jnp
from jax import lax
from jax.experimental import pallas as pl
from jax.experimental.pallas import tpu as pltpu
from jax.sharding import PartitionSpec as P

ITERS = 2
LANES = 128
PAD = 16
SPAN = 5
CHUNK = 32


def local_kernel(use_field, starts, field_ref, code_ref, jac_ref, null_ref, out_ref, hot_ref, row_ref):
    step = pl.program_id(0)

    @pl.when(step == 0)
    def _():
        out_ref[...] = jnp.zeros_like(out_ref)

    lane_iota = lax.broadcasted_iota(jnp.int32, (LANES, LANES), 0)
    codes = [code_ref[pl.ds(i, 1), :] for i in range(CHUNK)]
    begin = [starts[step * CHUNK + i] for i in range(CHUNK)]
    for i in range(CHUNK):
        hot = lane_iota == (codes[i] & (LANES - 1))
        hot_ref[i] = jnp.where(hot, 1.0, 0.0).astype(jnp.bfloat16)
    if use_field:
        for i in range(CHUNK):
            window = field_ref[pl.ds(begin[i], SPAN)].reshape(SPAN * PAD, LANES).astype(jnp.bfloat16)
            spots = jnp.dot(window, hot_ref[i], preferred_element_type=jnp.float32)
            part = codes[i] >> 7
            gathered = jnp.zeros((PAD, LANES), jnp.float32)
            for q in range(SPAN):
                gathered = jnp.where(part == q, spots[q * PAD:(q + 1) * PAD], gathered)
            jac = jac_ref[i].astype(jnp.float32)
            row_ref[pl.ds(i, 1), :] = jnp.sum(jac * gathered, axis=0, keepdims=True)
    else:
        row_ref[...] = jnp.where(code_ref[...] >= 0, field_ref[...].astype(jnp.float32), 0.0)
    inner = []
    for i in range(CHUNK):
        lifted = row_ref[pl.ds(i, 1), :].astype(jnp.bfloat16)
        inner.append(jnp.dot(lifted, null_ref[i], preferred_element_type=jnp.float32).astype(jnp.bfloat16))
    for i in range(CHUNK):
        row_ref[pl.ds(i, 1), :] = lax.dot_general(
            inner[i], null_ref[i], (((1,), (1,)), ((), ())), preferred_element_type=jnp.float32
        )
    back = []
    for i in range(CHUNK):
        part = codes[i] >> 7
        terms = jac_ref[i].astype(jnp.float32) * row_ref[pl.ds(i, 1), :]
        placed = jnp.concatenate(
            [jnp.where(part == q, terms, 0.0) for q in range(SPAN)], axis=0
        ).astype(jnp.bfloat16)
        back.append(lax.dot_general(
            placed, hot_ref[i], (((1,), (1,)), ((), ())), preferred_element_type=jnp.float32
        ).reshape(SPAN, PAD, LANES))
    for i in range(CHUNK):
        out_ref[pl.ds(begin[i], SPAN)] += back[i]


def local_terms(use_field, starts, field, code, jac, null, groups):
    blocks = null.shape[0]
    if use_field:
        source = pl.BlockSpec(field.shape, lambda b, s: (0, 0, 0))
    else:
        source = pl.BlockSpec((CHUNK, LANES), lambda b, s: (b, 0))
    return pl.pallas_call(
        functools.partial(local_kernel, use_field),
        grid_spec=pltpu.PrefetchScalarGridSpec(
            num_scalar_prefetch=1,
            grid=(blocks // CHUNK,),
            in_specs=[
                source,
                pl.BlockSpec((CHUNK, LANES), lambda b, s: (b, 0)),
                pl.BlockSpec((CHUNK, PAD, LANES), lambda b, s: (b, 0, 0)),
                pl.BlockSpec((CHUNK, LANES, LANES), lambda b, s: (b, 0, 0)),
            ],
            out_specs=pl.BlockSpec((groups, PAD, LANES), lambda b, s: (0, 0, 0)),
            scratch_shapes=[
                pltpu.VMEM((CHUNK, LANES, LANES), jnp.bfloat16),
                pltpu.VMEM((CHUNK, LANES), jnp.float32),
            ],
        ),
        out_shape=jax.ShapeDtypeStruct((groups, PAD, LANES), jnp.float32),
        name="local_field" if use_field else "local_gradient",
    )(starts, field, code, jac, null)


def remote(src, dst, send, recv, axis, index):
    return pltpu.make_async_remote_copy(
        src_ref=src, dst_ref=dst, send_sem=send, recv_sem=recv,
        device_id={axis: index}, device_id_type=pl.DeviceIdType.MESH,
    )


def greet(n, m):
    i, w = lax.axis_index("lm"), lax.axis_index("kf")
    barrier = pltpu.get_barrier_semaphore()
    for k in range(1, n):
        pl.semaphore_signal(
            barrier, inc=1, device_id={"lm": lax.rem(i + k, n)}, device_id_type=pl.DeviceIdType.MESH
        )
    for k in range(1, m):
        pl.semaphore_signal(
            barrier, inc=1, device_id={"kf": lax.rem(w + k, m)}, device_id_type=pl.DeviceIdType.MESH
        )
    pl.semaphore_wait(barrier, n - 1 + m - 1)


def reduce_spread(n, m, pair, h, full, bufs, sems):
    fold, acc, rs = bufs
    fold_s, fold_r, rs_s, rs_r, ag_s, ag_r, fw_s, fw_r = sems
    own = acc.shape[0]
    sh = own // n
    i, w = lax.axis_index("lm"), lax.axis_index("kf")
    later, former = lax.rem(w + 1, m), lax.rem(w + m - 1, m)

    def at(ref, j, base=0):
        return ref.at[pl.ds(base + j * sh, sh)]

    order = [lax.rem(i + k, n) for k in range(1, n)] + [i]
    others = order[:-1]
    folds = [remote(at(h, j, own), at(fold, j), fold_s.at[k], fold_r.at[k], "kf", later) for k, j in enumerate(order)]

    @pl.when(w < m - 1)
    def _():
        for copy in folds:
            copy.start()

    scatters = [remote(at(acc, j), rs.at[i], rs_s.at[k], rs_r.at[i], "lm", j) for k, j in enumerate(others)]
    for k, j in enumerate(order):
        spot = pl.ds(j * sh, sh)

        @pl.when(w > 0)
        def _():
            folds[k].wait_recv()
            acc[spot] = h[spot] + fold[spot]

        @pl.when(w == 0)
        def _():
            acc[spot] = h[spot]

        if k < n - 1:
            scatters[k].start()
    total = acc[pl.ds(i * sh, sh)]
    arrive = [lax.rem(i + n - k, n) for k in range(1, n)]
    for j in arrive:
        remote(at(acc, j), rs.at[j], rs_s.at[0], rs_r.at[j], "lm", j).wait_recv()
        total = total + rs[j]
    full[pl.ds(i * sh, sh)] = total
    gathers = [remote(at(full, i), at(full, i), ag_s.at[k], ag_r.at[i], "lm", j) for k, j in enumerate(others)]
    for copy in gathers:
        copy.start()
    forwards = []
    for k, j in enumerate([i] + arrive):
        if k > 0:
            remote(at(full, j), at(full, j), ag_s.at[0], ag_r.at[j], "lm", j).wait_recv()
        if pair:
            copy = remote(at(full, j), at(full, j, own), fw_s.at[k], fw_r.at[k], "kf", former)
            forwards.append(copy)

            @pl.when(w > 0)
            def _():
                copy.start()

    def finish_pair():
        @pl.when(w < m - 1)
        def _():
            for copy in forwards:
                copy.wait_recv()

        @pl.when(w == m - 1)
        def _():
            full[pl.ds(own, own)] = jnp.zeros((own,) + full.shape[1:], jnp.float32)

    def finish_sends():
        @pl.when(w < m - 1)
        def _():
            for copy in folds:
                copy.wait_send()

        for copy in scatters + gathers:
            copy.wait_send()
        if pair:

            @pl.when(w > 0)
            def _():
                for copy in forwards:
                    copy.wait_send()

    return finish_pair, finish_sends


def over_windows(m, value, slots, send, recv):
    w = lax.axis_index("kf")
    slots[w] = jnp.sum(value, axis=0)
    copies = []
    for k in range(1, m):
        copy = remote(slots.at[w], slots.at[w], send.at[k], recv.at[w], "kf", lax.rem(w + k, m))
        copy.start()
        copies.append(copy)
    for k in range(1, m):
        j = lax.rem(w + k, m)
        remote(slots.at[j], slots.at[j], send.at[0], recv.at[j], "kf", j).wait_recv()
    total = slots[0]
    for j in range(1, m):
        total = total + slots[j]

    def finish():
        for copy in copies:
            copy.wait_send()

    return jnp.sum(jnp.sum(total, axis=0, keepdims=True), axis=1, keepdims=True), finish


def columns(g):
    return pl.ds(g * LANES, LANES)


def first_phase(n, m, h, damping, jacobi_scale, res_out, dir_out, energy_out, diag_out, full, fold, acc, rs, slots, diag, *sems):
    own = acc.shape[0]
    state = damping.shape[0]
    w = lax.axis_index("kf")
    diag[...] = jnp.zeros_like(diag)
    for g in range(own):
        diag[g, pl.ds(0, state), :] = damping[:, columns(g)]
        diag[g, pl.ds(PAD, state), :] = jacobi_scale[:, columns(g)]
    greet(n, m)
    diag_copy = remote(
        diag.at[pl.ds(0, own)], diag.at[pl.ds(own, own)], sems[10].at[0], sems[10].at[1], "kf", lax.rem(w + m - 1, m)
    )

    @pl.when(w > 0)
    def _():
        diag_copy.start()

    finish_pair, finish_sends = reduce_spread(n, m, True, h, full, (fold, acc, rs), sems[:8])
    grad = full[pl.ds(0, own)]
    scale = diag[pl.ds(0, own), pl.ds(PAD, PAD), :]
    energy, finish = over_windows(m, grad * grad * scale, slots.at[0], sems[8].at[0], sems[9].at[0])
    energy_out[...] = jnp.broadcast_to(energy, energy_out.shape)
    finish_pair()

    @pl.when(w < m - 1)
    def _():
        diag_copy.wait_recv()

    @pl.when(w > 0)
    def _():
        diag_copy.wait_send()

    res_out[...] = -full[...]
    dir_out[...] = -full[...] * diag[:, pl.ds(PAD, PAD), :]
    diag_out[...] = diag[...]
    finish()
    finish_sends()


def middle_phase(begun, n, m, h, res, direction, diag, energy_in, *rest):
    if begun:
        answer_in, *rest = rest
    res_out, dir_out, energy_out, answer_out, full, fold, acc, rs, slots, *sems = rest
    own = acc.shape[0]
    here, damp, scale = pl.ds(0, own), pl.ds(0, PAD), pl.ds(PAD, PAD)
    greet(n, m)
    finish_pair, finish_sends = reduce_spread(n, m, True, h, full, (fold, acc, rs), sems[:8])
    energy = energy_in[pl.ds(0, 1), pl.ds(0, 1)]
    applied = full[here] + diag[here, damp, :] * direction[here]
    curve, finish_a = over_windows(m, direction[here] * applied, slots.at[0], sems[8].at[0], sems[9].at[0])
    step = energy / curve
    after = res[here] - step * applied
    fresh, finish_b = over_windows(m, after * after * diag[here, scale, :], slots.at[1], sems[8].at[1], sems[9].at[1])
    gained = step * direction[here]
    answer_out[...] = answer_in[...] + gained if begun else gained
    energy_out[...] = jnp.broadcast_to(fresh, energy_out.shape)
    finish_pair()
    after = res[...] - step * (full[...] + diag[:, damp, :] * direction[...])
    res_out[...] = after
    dir_out[...] = diag[:, scale, :] * after + fresh / energy * direction[...]
    finish_a()
    finish_b()
    finish_sends()


def last_phase(n, m, h, direction, diag, energy_in, applied_out, step_out, full, fold, acc, rs, slots, *sems):
    own = acc.shape[0]
    here = pl.ds(0, own)
    greet(n, m)
    _, finish_sends = reduce_spread(n, m, False, h, full, (fold, acc, rs), sems[:8])
    applied = full[here] + diag[here, pl.ds(0, PAD), :] * direction[here]
    applied_out[...] = applied
    curve, finish = over_windows(m, direction[here] * applied, slots.at[0], sems[8].at[0], sems[9].at[0])
    step = energy_in[pl.ds(0, 1), pl.ds(0, 1)] / curve
    step_out[...] = jnp.broadcast_to(step, step_out.shape)
    finish()
    finish_sends()


def update_kernel(res, direction, applied, answer_in, step_in, answer_out, res_out):
    own = applied.shape[0]
    state = res_out.shape[0]
    step = step_in[pl.ds(0, 1), pl.ds(0, 1)]
    for g in range(own):
        answer_out[:, columns(g)] = (answer_in[g] + step * direction[g])[:state]
        res_out[:, columns(g)] = (res[g] - step * applied[g])[:state]


def last_update(shape, res, direction, applied, answer, step):
    half = pl.BlockSpec(applied.shape, lambda i: (0, 0, 0))
    whole = pl.BlockSpec(shape, lambda i: (0, 0))
    return pl.pallas_call(
        update_kernel,
        grid=(1,),
        in_specs=[half] * 4 + [pl.BlockSpec(step.shape, lambda i: (0, 0))],
        out_specs=[whole] * 2,
        out_shape=[jax.ShapeDtypeStruct(shape, jnp.float32)] * 2,
        name="last_update",
    )(res, direction, applied, answer, step)


def phase(kernel, name, number, n, m, outs, extra, *operands):
    pair = operands[0].shape
    own = pair[0] // 2
    tile = pair[1:]
    vmem = pl.BlockSpec(memory_space=pltpu.VMEM)
    dma = pltpu.SemaphoreType.DMA
    return pl.pallas_call(
        functools.partial(kernel, n, m),
        in_specs=[vmem] * len(operands),
        out_specs=[vmem] * len(outs),
        out_shape=[jax.ShapeDtypeStruct(shape, jnp.float32) for shape in outs],
        scratch_shapes=[
            pltpu.VMEM(pair, jnp.float32),
            pltpu.VMEM((own,) + tile, jnp.float32),
            pltpu.VMEM((own,) + tile, jnp.float32),
            pltpu.VMEM((n, own // n) + tile, jnp.float32),
            pltpu.VMEM((2, m) + tile, jnp.float32),
        ]
        + [pltpu.VMEM(shape, jnp.float32) for shape in extra]
        + [dma((n,))] * 8
        + [dma((2, m))] * 2
        + [dma((2,))],
        compiler_params=pltpu.CompilerParams(collective_id=number, has_side_effects=True),
        name=name,
    )(*operands)


def prepare(frame_ids, obs_count, first_frame, groups):
    rel = frame_ids - first_frame
    starts = jnp.minimum(rel[:, 0] // LANES, groups - SPAN)
    slots = lax.broadcasted_iota(jnp.int32, rel.shape, 1)
    off = jnp.where(slots < obs_count[:, None], rel - starts[:, None] * LANES, -1)
    twice = (
        lax.broadcasted_iota(jnp.int32, (rel.shape[1], 2 * rel.shape[1]), 0)
        == lax.broadcasted_iota(jnp.int32, (rel.shape[1], 2 * rel.shape[1]), 1) // 2
    ).astype(jnp.float32)
    code = jnp.dot(off.astype(jnp.float32), twice, precision=lax.Precision.HIGHEST)
    return starts, jnp.round(code).astype(jnp.int32)


def shards(residual_rows, jacobian, nullspace, frame_ids, obs_count, damping, jacobi_scale):
    state, frames = damping.shape
    own = frames // LANES
    starts, code = prepare(frame_ids, obs_count, lax.axis_index("kf") * frames, 2 * own)
    jac = jnp.pad(jacobian, ((0, 0), (0, PAD - state), (0, 0)))
    n, m = lax.axis_size("lm"), lax.axis_size("kf")
    pair, one, tile = (2 * own, PAD, LANES), (own, PAD, LANES), (8, LANES)
    both = (2 * own, 2 * PAD, LANES)

    def product(field):
        return local_terms(True, starts, field, code, jac, nullspace, 2 * own)

    gradient = local_terms(False, starts, residual_rows, code, jac, nullspace, 2 * own)
    residual, direction, energy, diag = phase(
        first_phase, "first_phase", 0, n, m, (pair, pair, tile, both), (both,), gradient, damping, jacobi_scale
    )
    answer = ()
    for number in range(1, ITERS):
        residual, direction, energy, *answer = phase(
            functools.partial(middle_phase, number > 1), "middle_phase", number, n, m, (pair, pair, tile, one), (),
            product(direction), residual, direction, diag, energy, *answer,
        )
    applied, step = phase(
        last_phase, "last_phase", ITERS, n, m, (one, tile), (), product(direction), direction, diag, energy
    )
    return tuple(last_update(damping.shape, residual, direction, applied, *answer, step))


def solution(mesh):
    placed = (
        P(("lm", "kf"), None),
        P(("lm", "kf"), None, None),
        P(("lm", "kf"), None, None),
        P(("lm", "kf"), None),
        P(("lm", "kf")),
        P(None, "kf"),
        P(None, "kf"),
    )
    return jax.shard_map(
        shards,
        mesh=mesh,
        in_specs=placed,
        out_specs=(P(None, "kf"), P(None, "kf")),
        check_vma=False,
    )
```

profile of v0, /device:TPU:0, one launch (start us, length us, event | category | flops | bytes accessed | tf_op | source)
XLA Modules:
  0.0 122.3 jit_solution(6896648907478622695)
XLA Ops:
  0.7 0.8 broadcast_subtract_fusion
  1.4 0.5 fusion.10.starts
  2.0 1.5 %fusion.code_ref = s32[128,128]{1,0:T(8,128)} fusion(s32[128,64]{0,1:T(8,128)S(1)} %broadcast_subtract_fusion, s32[128]{0:T(128)S(1)} %get-tuple-element.22, s32[128]{0:T(128)S(1)} %get-tuple-element.23, s32[128]{0:T(128)S(1)} %multiply_bitcast_fusion, s32[128]{0:T(128)} %param.11, pred[128]{0:T(512)(128)(4,1)S(1)} %compare_and_fusion), kind=kOutput, calls=%fused_computation.1 | convolution fusion | flops 12664832 | bytes 100480 | tf_op jit(solution)/shard_map/dot_general | solution.py:360
  3.5 1.4 %copy.9 = bf16[128,15,128]{2,1,0:T(8,128)(2,1)S(1)} copy(bf16[128,15,128]{2,0,1:T(8,128)(2,1)} %param.8) | data formatting | bytes 983040 | tf_op args[1]
  4.9 0.9 pad.4.jac_ref
  5.8 9.6 %local_gradient.1.h = f32[64,16,128]{2,1,0:T(8,128)} custom-call(s32[128]{0:T(128)} %fusion.10.starts, bf16[128,128]{1,0:T(8,128)(2,1)} %field_ref.1, s32[128,128]{1,0:T(8,128)} %fusion.code_ref, bf16[128,16,128]{2,1,0:T(8,128)(2,1)} %pad.4.jac_ref, bf16[128,128,128]{2,1,0:T(8,128)(2,1)} %null_ref.5), custom_call_target="tpu_custom_call" | custom-call | tf_op jit(solution)/shard_map/local_gradient/pallas_call | solution.py:70
  15.4 29.0 %first_phase.1 = (f32[64,16,128]{2,1,0:T(8,128)}, f32[64,16,128]{2,1,0:T(8,128)}, f32[8,128]{1,0:T(8,128)}, f32[64,32,128]{2,1,0:T(8,128)}) custom-call(f32[64,16,128]{2,1,0:T(8,128)} %local_gradient.1.h, f32[15,4096]{1,0:T(8,128)} %damping.1, f32[15,4096]{1,0:T(8,128)} %jacobi_scale.1), custom_call_target="tpu_custom_call" | custom-call | tf_op jit(solution)/shard_map/first_phase/pallas_call | solution.py:330
  44.4 11.6 %local_field.2.h = f32[64,16,128]{2,1,0:T(8,128)} custom-call(s32[128]{0:T(128)} %fusion.10.starts, f32[64,16,128]{2,1,0:T(8,128)} %get-tuple-element.12.field_ref.direction, s32[128,128]{1,0:T(8,128)} %fusion.code_ref, bf16[128,16,128]{2,1,0:T(8,128)(2,1)} %pad.4.jac_ref, bf16[128,128,128]{2,1,0:T(8,128)(2,1)} %null_ref.5), custom_call_target="tpu_custom_call" | custom-call | tf_op jit(solution)/shard_map/local_field/pallas_call | solution.py:70
  56.0 28.7 %middle_phase.1 = (f32[64,16,128]{2,1,0:T(8,128)}, f32[64,16,128]{2,1,0:T(8,128)}, f32[8,128]{1,0:T(8,128)}, f32[32,16,128]{2,1,0:T(8,128)}) custom-call(f32[64,16,128]{2,1,0:T(8,128)} %local_field.2.h, f32[64,16,128]{2,1,0:T(8,128)} %get-tuple-element.13.res, f32[64,16,128]{2,1,0:T(8,128)} %get-tuple-element.12.field_ref.direction, ...), custom_call_target="tpu_custom_call" | custom-call | tf_op jit(solution)/shard_map/middle_phase/pallas_call | solution.py:330
  84.7 11.6 %local_field.3.h = f32[64,16,128]{2,1,0:T(8,128)} custom-call(s32[128]{0:T(128)} %fusion.10.starts, f32[64,16,128]{2,1,0:T(8,128)} %get-tuple-element.17.field_ref.direction, s32[128,128]{1,0:T(8,128)} %fusion.code_ref, bf16[128,16,128]{2,1,0:T(8,128)(2,1)} %pad.4.jac_ref, bf16[128,128,128]{2,1,0:T(8,128)(2,1)} %null_ref.5), custom_call_target="tpu_custom_call" | custom-call | tf_op jit(solution)/shard_map/local_field/pallas_call | solution.py:70
  96.3 23.9 %last_phase.1 = (f32[32,16,128]{2,1,0:T(8,128)}, f32[8,128]{1,0:T(8,128)}) custom-call(f32[64,16,128]{2,1,0:T(8,128)} %local_field.3.h, f32[64,16,128]{2,1,0:T(8,128)} %get-tuple-element.17.field_ref.direction, f32[64,32,128]{2,1,0:T(8,128)} %get-tuple-element.14.diag, f32[8,128]{1,0:T(8,128)} %get-tuple-element.18.energy_in), custom_call_target="tpu_custom_call" | custom-call | tf_op jit(solution)/shard_map/last_phase/pallas_call | solution.py:330
  120.2 2.1 %last_update.1 = (f32[15,4096]{1,0:T(8,128)}, f32[15,4096]{1,0:T(8,128)}) custom-call(f32[64,16,128]{2,1,0:T(8,128)} %get-tuple-element.16.res, f32[64,16,128]{2,1,0:T(8,128)} %get-tuple-element.17.field_ref.direction, f32[32,16,128]{2,1,0:T(8,128)} %get-tuple-element.19.applied, f32[32,16,128]{2,1,0:T(8,128)} %get-tuple-element.20.answer_in, ...), custom_call_target="tpu_custom_call" | custom-call | tf_op jit(solution)/shard_map/last_update/pallas_call | solution.py:314
  (3 shorter events, 0.0 us)
where the time goes:
time: 123 us; the launch traced here: 122 us
  Pallas kernels  116 us (94%)
  local copies, waits for them, and re-layouts  2.26 us (2%)
  matrix products  1.55 us (1%)
  other arithmetic  1.31 us (1%)
    pallas_call x3, Pallas kernels, phase(): pl.pallas_call(functools.partial(kernel, n, m), in_specs=[vmem] * len(ope...  81.7 us
    pallas_call x3, Pallas kernels, local_terms(): pl.pallas_call(functools.partial(local_kernel, use_field), grid_spec=pltp...  32.8 us

commit v1 on v0

--- a/solution.py
+++ b/solution.py
@@ -12,81 +12,154 @@
 PAD = 16
 SPAN = 5
 CHUNK = 32
-
-
-def local_kernel(use_field, starts, field_ref, code_ref, jac_ref, null_ref, out_ref, hot_ref, row_ref):
-    step = pl.program_id(0)
-
-    @pl.when(step == 0)
-    def _():
-        out_ref[...] = jnp.zeros_like(out_ref)
-
-    lane_iota = lax.broadcasted_iota(jnp.int32, (LANES, LANES), 0)
-    codes = [code_ref[pl.ds(i, 1), :] for i in range(CHUNK)]
-    begin = [starts[step * CHUNK + i] for i in range(CHUNK)]
-    for i in range(CHUNK):
-        hot = lane_iota == (codes[i] & (LANES - 1))
-        hot_ref[i] = jnp.where(hot, 1.0, 0.0).astype(jnp.bfloat16)
-    if use_field:
+PICK = 8
+DEAD = 1 << 20
+LIMIT = 16 << 20
+
+
+def spread_over(lifted, factors, first):
+    picks = lax.broadcasted_iota(jnp.int32, lifted.shape, 0)
+    half = lifted.astype(jnp.bfloat16)
+    inner = jnp.zeros(lifted.shape, jnp.float32)
+    for i in range(PICK):
+        inner = jnp.where(picks == i, jnp.dot(half, factors[first + i], preferred_element_type=jnp.float32), inner)
+    half = inner.astype(jnp.bfloat16)
+    spread = jnp.zeros(lifted.shape, jnp.float32)
+    for i in range(PICK):
+        spread = jnp.where(
+            picks == i,
+            lax.dot_general(
+                half, factors[first + i], (((1,), (1,)), ((), ())), preferred_element_type=jnp.float32
+            ),
+            spread,
+        )
+    return spread
+
+
+def sums_of_eight(tiles):
+    rows = lax.broadcasted_iota(jnp.int32, tiles[0].shape, 0)
+    width = 1
+    while width < PICK:
+        low = (rows & width) == 0
+        tiles = [
+            jnp.where(low, left, right) + pltpu.roll(jnp.where(low, right, left), width, axis=0)
+            for left, right in zip(tiles[::2], tiles[1::2])
+        ]
+        width *= 2
+    return tiles[0]
+
+
+def along_lanes(tile, lanes):
+    return jnp.take_along_axis(tile, lanes, axis=1, mode="promise_in_bounds")
+
+
+def scatter_terms(starts, block, i, jac, row_ref, inv_ref, out_ref, even):
+    terms = jac * row_ref[pl.ds(i, 1), :]
+    terms = jnp.where(even, terms + pltpu.roll(terms, LANES - 1, axis=1), 0.0)
+    begin = starts[block]
+    for q in range(SPAN):
+        lanes = jnp.broadcast_to(inv_ref[i, pl.ds(q, 1), :], terms.shape)
+        out_ref[begin + q] += along_lanes(terms, lanes)
+
+
+def even_lanes():
+    return (lax.broadcasted_iota(jnp.int32, (PAD, LANES), 1) & 1) == 0
+
+
+def product_kernel(starts, field_ref, code_ref, inv_ref, jac_ref, null_ref, out_ref, row_ref):
+    out_ref[...] = jnp.zeros_like(out_ref)
+    even = even_lanes()
+
+    @pl.loop(0, null_ref.shape[0] // CHUNK)
+    def _(step):
+        base = pl.multiple_of(step * CHUNK, CHUNK)
+        mine = pl.ds(base, CHUNK)
+        codes, invs, jacs, factors = code_ref.at[mine], inv_ref.at[mine], jac_ref.at[mine], null_ref.at[mine]
+        for first in range(0, CHUNK, PICK):
+            tiles = []
+            for i in range(first, first + PICK):
+                begin = starts[base + i]
+                code = jnp.broadcast_to(codes[pl.ds(i, 1), :], (PAD, LANES))
+                lanes, part = code & (LANES - 1), code >> 7
+                gathered = jnp.zeros((PAD, LANES), jnp.float32)
+                for q in range(SPAN):
+                    gathered = jnp.where(part == q, along_lanes(field_ref[begin + q], lanes), gathered)
+                gathered = gathered * jacs[i]
+                tiles.append(gathered[:PICK] + gathered[PICK:])
+            row_ref[pl.ds(first, PICK), :] = spread_over(sums_of_eight(tiles), factors, first)
         for i in range(CHUNK):
-            window = field_ref[pl.ds(begin[i], SPAN)].reshape(SPAN * PAD, LANES).astype(jnp.bfloat16)
-            spots = jnp.dot(window, hot_ref[i], preferred_element_type=jnp.float32)
-            part = codes[i] >> 7
-            gathered = jnp.zeros((PAD, LANES), jnp.float32)
-            for q in range(SPAN):
-                gathered = jnp.where(part == q, spots[q * PAD:(q + 1) * PAD], gathered)
-            jac = jac_ref[i].astype(jnp.float32)
-            row_ref[pl.ds(i, 1), :] = jnp.sum(jac * gathered, axis=0, keepdims=True)
-    else:
-        row_ref[...] = jnp.where(code_ref[...] >= 0, field_ref[...].astype(jnp.float32), 0.0)
-    inner = []
-    for i in range(CHUNK):
-        lifted = row_ref[pl.ds(i, 1), :].astype(jnp.bfloat16)
-        inner.append(jnp.dot(lifted, null_ref[i], preferred_element_type=jnp.float32).astype(jnp.bfloat16))
-    for i in range(CHUNK):
-        row_ref[pl.ds(i, 1), :] = lax.dot_general(
-            inner[i], null_ref[i], (((1,), (1,)), ((), ())), preferred_element_type=jnp.float32
-        )
-    back = []
-    for i in range(CHUNK):
-        part = codes[i] >> 7
-        terms = jac_ref[i].astype(jnp.float32) * row_ref[pl.ds(i, 1), :]
-        placed = jnp.concatenate(
-            [jnp.where(part == q, terms, 0.0) for q in range(SPAN)], axis=0
-        ).astype(jnp.bfloat16)
-        back.append(lax.dot_general(
-            placed, hot_ref[i], (((1,), (1,)), ((), ())), preferred_element_type=jnp.float32
-        ).reshape(SPAN, PAD, LANES))
-    for i in range(CHUNK):
-        out_ref[pl.ds(begin[i], SPAN)] += back[i]
-
-
-def local_terms(use_field, starts, field, code, jac, null, groups):
-    blocks = null.shape[0]
-    if use_field:
-        source = pl.BlockSpec(field.shape, lambda b, s: (0, 0, 0))
-    else:
-        source = pl.BlockSpec((CHUNK, LANES), lambda b, s: (b, 0))
+            scatter_terms(starts, base + i, i, jacs[i], row_ref, invs, out_ref, even)
+
+
+def gradient_kernel(
+    starts, ids_ref, count_ref, rows_ref, jac_in, null_in,
+    out_ref, code_ref, inv_ref, jac_ref, null_ref, row_ref, slot_ref, sems,
+):
+    blocks = null_ref.shape[0]
+    chunks = blocks // CHUNK
+    copies = []
+    for c in range(chunks):
+        mine = pl.ds(c * CHUNK, CHUNK)
+        copies.append(pltpu.make_async_copy(null_in.at[mine], null_ref.at[mine], sems.at[c]))
+        copies[c].start()
+    out_ref[...] = jnp.zeros_like(out_ref)
+    frames = out_ref.shape[0] // 2 * LANES
+    ids = ids_ref[...] - lax.axis_index("kf") * frames
+    begin = jnp.minimum(ids[:1] >> 7, out_ref.shape[0] - SPAN)
+    slots = lax.broadcasted_iota(jnp.int32, ids.shape, 0)
+    ids = jnp.where(slots < count_ref[...], ids - begin * LANES, DEAD)
+    offs = jnp.transpose(jnp.concatenate([ids] * (LANES // ids.shape[0]), axis=0))
+    slot_ref[...] = offs
+    lanes = lax.broadcasted_iota(jnp.int32, offs.shape, 1)
+    code_ref[...] = along_lanes(offs, lanes >> 1)
+    state = jac_in.shape[0]
+    for c in range(PAD):
+        for g in range(blocks // PICK):
+            spot = pl.ds(g * PICK * PAD + c, PICK, stride=PAD)
+            if c < state:
+                jac_ref[spot, :] = jac_in[c, pl.ds(g * PICK, PICK), :].astype(jnp.float32)
+            else:
+                jac_ref[spot, :] = jnp.zeros((PICK, LANES), jnp.float32)
+    even = even_lanes()
+    tile = (PICK, LANES)
+    target = lax.broadcasted_iota(jnp.int32, tile, 0) * LANES + lax.broadcasted_iota(jnp.int32, tile, 1)
+    for c in range(chunks):
+        copies[c].wait()
+
+    @pl.loop(0, chunks)
+    def _(step):
+        base = pl.multiple_of(step * CHUNK, CHUNK)
+        mine = pl.ds(base, CHUNK)
+        codes, invs, factors = code_ref.at[mine], inv_ref.at[mine], null_ref.at[mine]
+        offsets = slot_ref.at[mine]
+        jacs = jac_ref.at[pl.ds(pl.multiple_of(step * CHUNK * PAD, CHUNK * PAD), CHUNK * PAD)]
+        residuals = rows_ref[mine, :].astype(jnp.float32)
+        lifted = jnp.where(codes[...] < DEAD, residuals, 0.0)
+        for first in range(0, CHUNK, PICK):
+            row_ref[pl.ds(first, PICK), :] = spread_over(lifted[first:first + PICK], factors, first)
+        for i in range(CHUNK):
+            offset = jnp.broadcast_to(offsets[pl.ds(i, 1), :], tile)
+            at = jnp.zeros(tile, jnp.int32)
+            width = ids_ref.shape[0] // 2
+            while width > 0:
+                at = jnp.where(along_lanes(offset, at + width) <= target, at + width, at)
+                width //= 2
+            invs[i] = jnp.where(along_lanes(offset, at) == target, 2 * at, LANES - 1)
+        for i in range(CHUNK):
+            scatter_terms(starts, base + i, i, jacs[pl.ds(i * PAD, PAD), :], row_ref, invs, out_ref, even)
+
+
+def local_call(kernel, name, outs, extra, in_specs, *operands):
+    vmem = pl.BlockSpec(memory_space=pltpu.VMEM)
     return pl.pallas_call(
-        functools.partial(local_kernel, use_field),
-        grid_spec=pltpu.PrefetchScalarGridSpec(
-            num_scalar_prefetch=1,
-            grid=(blocks // CHUNK,),
-            in_specs=[
-                source,
-                pl.BlockSpec((CHUNK, LANES), lambda b, s: (b, 0)),
-                pl.BlockSpec((CHUNK, PAD, LANES), lambda b, s: (b, 0, 0)),
-                pl.BlockSpec((CHUNK, LANES, LANES), lambda b, s: (b, 0, 0)),
-            ],
-            out_specs=pl.BlockSpec((groups, PAD, LANES), lambda b, s: (0, 0, 0)),
-            scratch_shapes=[
-                pltpu.VMEM((CHUNK, LANES, LANES), jnp.bfloat16),
-                pltpu.VMEM((CHUNK, LANES), jnp.float32),
-            ],
-        ),
-        out_shape=jax.ShapeDtypeStruct((groups, PAD, LANES), jnp.float32),
-        name="local_field" if use_field else "local_gradient",
-    )(starts, field, code, jac, null)
+        kernel,
+        in_specs=[pl.BlockSpec(memory_space=pltpu.SMEM)] + in_specs,
+        out_specs=[vmem] * len(outs),
+        out_shape=outs,
+        scratch_shapes=[pltpu.VMEM((CHUNK, LANES), jnp.float32)] + extra,
+        compiler_params=pltpu.CompilerParams(vmem_limit_bytes=LIMIT),
+        name=name,
+    )(*operands)
 
 
 def remote(src, dst, send, recv, axis, index):
@@ -317,6 +390,7 @@
         in_specs=[half] * 4 + [pl.BlockSpec(step.shape, lambda i: (0, 0))],
         out_specs=[whole] * 2,
         out_shape=[jax.ShapeDtypeStruct(shape, jnp.float32)] * 2,
+        compiler_params=pltpu.CompilerParams(vmem_limit_bytes=LIMIT),
         name="last_update",
     )(res, direction, applied, answer, step)
 
@@ -343,37 +417,42 @@
         + [dma((n,))] * 8
         + [dma((2, m))] * 2
         + [dma((2,))],
-        compiler_params=pltpu.CompilerParams(collective_id=number, has_side_effects=True),
+        compiler_params=pltpu.CompilerParams(collective_id=number, has_side_effects=True, vmem_limit_bytes=LIMIT),
         name=name,
     )(*operands)
-
-
-def prepare(frame_ids, obs_count, first_frame, groups):
-    rel = frame_ids - first_frame
-    starts = jnp.minimum(rel[:, 0] // LANES, groups - SPAN)
-    slots = lax.broadcasted_iota(jnp.int32, rel.shape, 1)
-    off = jnp.where(slots < obs_count[:, None], rel - starts[:, None] * LANES, -1)
-    twice = (
-        lax.broadcasted_iota(jnp.int32, (rel.shape[1], 2 * rel.shape[1]), 0)
-        == lax.broadcasted_iota(jnp.int32, (rel.shape[1], 2 * rel.shape[1]), 1) // 2
-    ).astype(jnp.float32)
-    code = jnp.dot(off.astype(jnp.float32), twice, precision=lax.Precision.HIGHEST)
-    return starts, jnp.round(code).astype(jnp.int32)
 
 
 def shards(residual_rows, jacobian, nullspace, frame_ids, obs_count, damping, jacobi_scale):
     state, frames = damping.shape
     own = frames // LANES
-    starts, code = prepare(frame_ids, obs_count, lax.axis_index("kf") * frames, 2 * own)
-    jac = jnp.pad(jacobian, ((0, 0), (0, PAD - state), (0, 0)))
+    blocks = nullspace.shape[0]
+    starts = jnp.minimum((frame_ids[:, 0] - lax.axis_index("kf") * frames) >> 7, 2 * own - SPAN)
     n, m = lax.axis_size("lm"), lax.axis_size("kf")
     pair, one, tile = (2 * own, PAD, LANES), (own, PAD, LANES), (8, LANES)
     both = (2 * own, 2 * PAD, LANES)
+    vmem = pl.BlockSpec(memory_space=pltpu.VMEM)
+    gradient, code, inverse, jac, null = local_call(
+        gradient_kernel, "local_gradient",
+        [
+            jax.ShapeDtypeStruct(pair, jnp.float32),
+            jax.ShapeDtypeStruct((blocks, LANES), jnp.int32),
+            jax.ShapeDtypeStruct((blocks, PICK, LANES), jnp.int32),
+            jax.ShapeDtypeStruct((blocks * PAD, LANES), jnp.float32),
+            jax.ShapeDtypeStruct(nullspace.shape, nullspace.dtype),
+        ],
+        [pltpu.VMEM((blocks, LANES), jnp.int32), pltpu.SemaphoreType.DMA((blocks // CHUNK,))],
+        [vmem] * 4 + [pl.BlockSpec(memory_space=pltpu.HBM)],
+        starts, jnp.transpose(frame_ids), obs_count[None, :], residual_rows,
+        jnp.transpose(jacobian, (1, 0, 2)), nullspace,
+    )
+    jac = jac.reshape(blocks, PAD, LANES)
 
     def product(field):
-        return local_terms(True, starts, field, code, jac, nullspace, 2 * own)
-
-    gradient = local_terms(False, starts, residual_rows, code, jac, nullspace, 2 * own)
+        return local_call(
+            product_kernel, "local_field", [jax.ShapeDtypeStruct(pair, jnp.float32)], [], [vmem] * 5,
+            starts, field, code, inverse, jac, null,
+        )[0]
+
     residual, direction, energy, diag = phase(
         first_phase, "first_phase", 0, n, m, (pair, pair, tile, both), (both,), gradient, damping, jacobi_scale
     )

time: 123 us -> 108 us (0.88)
  Pallas kernels: 116 us -> 101 us
  local copies, waits for them, and re-layouts: 2.26 us -> 5.39 us
  matrix products: 1.55 us -> 0 us
    pallas_call x3, Pallas kernels: 81.7 us -> 74.3 us  [phase(): pl.pallas_call(functools.partial(kernel, n, m), in_specs=[vmem] * len(ope...]
    pallas_call x3, Pallas kernels: 32.8 us -> 25.6 us  [local_call(): pl.pallas_call(kernel, in_specs=[pl.BlockSpec(memory_space=pltpu.SMEM)] +...]
    unnamed x1 -> x14, local copies, waits for them, and re-layouts: 1.35 us -> 5.39 us
    dot_general x1 -> x0, matrix products: 1.55 us -> none  [prepare(): jnp.dot(off.astype(jnp.float32), twice, precision=lax.Precision.HIGHEST)]
where the time goes in v1:
time: 108 us
  Pallas kernels  101 us (94%)
  local copies, waits for them, and re-layouts  5.39 us (5%)
    pallas_call x3, Pallas kernels, phase(): pl.pallas_call(functools.partial(kernel, n, m), in_specs=[vmem] * len(ope...  74.3 us
    pallas_call x3, Pallas kernels, local_call(): pl.pallas_call(kernel, in_specs=[pl.BlockSpec(memory_space=pltpu.SMEM)] +...  25.6 us
    unnamed x14, local copies, waits for them, and re-layouts  5.39 us

profile of v1, /device:TPU:0, one launch (start us, length us, event | category | flops | bytes accessed | tf_op | source)
XLA Modules:
  0.0 107.6 jit_solution(2106090928608123347)
XLA Ops:
  0.6 0.7 minimum_bitcast_fusion.starts
  1.3 0.0 copy-start
  1.3 2.2 %copy-done = bf16[128,128,128]{2,1,0:T(8,128)(2,1)S(1)} copy-done((bf16[128,128,128]{2,1,0:T(8,128)(2,1)S(1)}, bf16[128,128,128]{2,1,0:T(8,128)(2,1)}, u32[]{:S(2)}) %copy-start) | copy-done | bytes 4194328
  3.5 0.0 copy-start.1
  3.5 1.0 copy-done.1
  4.5 0.0 copy-start.4
  4.5 0.8 copy-done.4
  5.3 0.0 copy-start.5
  5.3 0.8 copy-done.5
  6.1 0.0 copy-start.6
  6.1 0.7 copy-done.6
  6.7 0.0 copy-start.2
  6.7 0.0 copy-start.3
  6.7 9.6 %local_gradient.1 = (f32[64,16,128]{2,1,0:T(8,128)S(1)}, s32[128,128]{1,0:T(8,128)S(1)}, s32[128,8,128]{2,1,0:T(8,128)S(1)}, f32[2048,128]{1,0:T(8,128)S(1)}, bf16[128,128,128]{2,1,0:T(8,128)(2,1)S(1)}) custom-call(s32[128]{0:T(128)S(1)} %minimum_bitcast_fusion.starts, s32[64,128]{1,0:T(8,128)S(1)} %bitcast.9, s32[1,128]{1,0:T(1,128)S(1)} %bitcast.10, ...), custom_call_target="tpu_custom_call" | custom-call | tf_op jit(solution)/shard_map/local_gradient/pallas_call | solution.py:154
  16.3 0.0 copy-done.2
  16.3 0.0 copy-done.3
  16.3 26.5 %first_phase.1 = (f32[64,16,128]{2,1,0:T(8,128)S(1)}, f32[64,16,128]{2,1,0:T(8,128)S(1)}, f32[8,128]{1,0:T(8,128)S(1)}, f32[64,32,128]{2,1,0:T(8,128)S(1)}) custom-call(f32[64,16,128]{2,1,0:T(8,128)S(1)} %get-tuple-element.17.h, f32[15,4096]{1,0:T(8,128)S(1)} %copy-done.2, f32[15,4096]{1,0:T(8,128)S(1)} %copy-done.3), custom_call_target="tpu_custom_call" | custom-call | tf_op jit(solution)/shard_map/first_phase/pallas_call | solution.py:404
  42.8 8.0 %local_field.2.h = f32[64,16,128]{2,1,0:T(8,128)S(1)} custom-call(s32[128]{0:T(128)S(1)} %minimum_bitcast_fusion.starts, f32[64,16,128]{2,1,0:T(8,128)S(1)} %get-tuple-element.18.field_ref.direction, s32[128,128]{1,0:T(8,128)S(1)} %get-tuple-element.19.code_ref, s32[128,8,128]{2,1,0:T(8,128)S(1)} %get-tuple-element.20.inv_ref, f32[128,16,128]{2,1,0:T(8,128)S(1)} %bitcast.6, ...), custom_call_target="tpu_custom_call" | custom-call | tf_op jit(solution)/shard_map/local_field/pallas_call | solution.py:154
  50.8 26.0 %middle_phase.1 = (f32[64,16,128]{2,1,0:T(8,128)S(1)}, f32[64,16,128]{2,1,0:T(8,128)S(1)}, f32[8,128]{1,0:T(8,128)S(1)}, f32[32,16,128]{2,1,0:T(8,128)S(1)}) custom-call(f32[64,16,128]{2,1,0:T(8,128)S(1)} %local_field.2.h, f32[64,16,128]{2,1,0:T(8,128)S(1)} %get-tuple-element.23.res, f32[64,16,128]{2,1,0:T(8,128)S(1)} %get-tuple-element.18.field_ref.direction, ...), custom_call_target="tpu_custom_call" | custom-call | tf_op jit(solution)/shard_map/middle_phase/pallas_call | solution.py:404
  76.8 8.0 %local_field.3.h = f32[64,16,128]{2,1,0:T(8,128)S(1)} custom-call(s32[128]{0:T(128)S(1)} %minimum_bitcast_fusion.starts, f32[64,16,128]{2,1,0:T(8,128)S(1)} %get-tuple-element.27.field_ref.direction, s32[128,128]{1,0:T(8,128)S(1)} %get-tuple-element.19.code_ref, s32[128,8,128]{2,1,0:T(8,128)S(1)} %get-tuple-element.20.inv_ref, f32[128,16,128]{2,1,0:T(8,128)S(1)} %bitcast.7, ...), custom_call_target="tpu_custom_call" | custom-call | tf_op jit(solution)/shard_map/local_field/pallas_call | solution.py:154
  84.8 21.9 %last_phase.1 = (f32[32,16,128]{2,1,0:T(8,128)S(1)}, f32[8,128]{1,0:T(8,128)S(1)}) custom-call(f32[64,16,128]{2,1,0:T(8,128)S(1)} %local_field.3.h, f32[64,16,128]{2,1,0:T(8,128)S(1)} %get-tuple-element.27.field_ref.direction, f32[64,32,128]{2,1,0:T(8,128)S(1)} %get-tuple-element.24.diag, f32[8,128]{1,0:T(8,128)S(1)} %get-tuple-element.28.energy_in), custom_call_target="tpu_custom_call" | custom-call | tf_op jit(solution)/shard_map/last_phase/pallas_call | solution.py:404
  106.7 0.9 last_update.1
Async XLA Ops:
  1.3 2.2 %copy-start = (bf16[128,128,128]{2,1,0:T(8,128)(2,1)S(1)}, bf16[128,128,128]{2,1,0:T(8,128)(2,1)}, u32[]{:S(2)}) copy-start(bf16[128,128,128]{2,1,0:T(8,128)(2,1)} %null_in.1) | copy-start | bytes 12582916
  3.5 1.0 copy-start.1
  4.5 0.8 copy-start.4
  5.3 0.8 copy-start.5
  6.1 0.7 copy-start.6
  6.7 9.6 %copy-start.2 = (f32[15,4096]{1,0:T(8,128)S(1)}, f32[15,4096]{1,0:T(8,128)}, u32[]{:S(2)}) copy-start(f32[15,4096]{1,0:T(8,128)} %damping.1) | copy-start | bytes 737284
  6.7 9.6 %copy-start.3 = (f32[15,4096]{1,0:T(8,128)S(1)}, f32[15,4096]{1,0:T(8,128)}, u32[]{:S(2)}) copy-start(f32[15,4096]{1,0:T(8,128)} %jacobi_scale.1) | copy-start | bytes 737284

commit v2 on v1

--- a/solution.py
+++ b/solution.py
@@ -169,23 +169,32 @@
     )
 
 
+def partner(i, k):
+    bit, flipped = 1, i * 0
+    while bit <= k or bit == 1:
+        digit = lax.rem(i // bit, 2)
+        flipped = flipped + bit * ((1 - 2 * digit) if k & bit else 0)
+        bit *= 2
+    return i + flipped
+
+
 def greet(n, m):
     i, w = lax.axis_index("lm"), lax.axis_index("kf")
     barrier = pltpu.get_barrier_semaphore()
-    for k in range(1, n):
+    for k in range(n - 1, 0, -1):
         pl.semaphore_signal(
-            barrier, inc=1, device_id={"lm": lax.rem(i + k, n)}, device_id_type=pl.DeviceIdType.MESH
+            barrier, inc=1, device_id={"lm": partner(i, k)}, device_id_type=pl.DeviceIdType.MESH
         )
     for k in range(1, m):
         pl.semaphore_signal(
             barrier, inc=1, device_id={"kf": lax.rem(w + k, m)}, device_id_type=pl.DeviceIdType.MESH
         )
-    pl.semaphore_wait(barrier, n - 1 + m - 1)
-
-
-def reduce_spread(n, m, pair, h, full, bufs, sems):
-    fold, acc, rs = bufs
-    fold_s, fold_r, rs_s, rs_r, ag_s, ag_r, fw_s, fw_r = sems
+    return lambda: pl.semaphore_wait(barrier, n - 1 + m - 1)
+
+
+def all_reduce(n, m, pair, h, full, bufs, sems, on_shard):
+    fold, acc, rs, near, far = bufs
+    fold_s, fold_r, rs_s, rs_r, ag_s, ag_r, fw_s, fw_r, near_s, near_r, far_s, far_r = sems
     own = acc.shape[0]
     sh = own // n
     i, w = lax.axis_index("lm"), lax.axis_index("kf")
@@ -194,18 +203,20 @@
     def at(ref, j, base=0):
         return ref.at[pl.ds(base + j * sh, sh)]
 
-    order = [lax.rem(i + k, n) for k in range(1, n)] + [i]
-    others = order[:-1]
-    folds = [remote(at(h, j, own), at(fold, j), fold_s.at[k], fold_r.at[k], "kf", later) for k, j in enumerate(order)]
+    peers = [partner(i, k) for k in range(n)]
+    outward = range(n - 1, 0, -1)
+    folds = {
+        k: remote(at(h, peers[k], own), at(fold, peers[k]), fold_s.at[k], fold_r.at[k], "kf", later) for k in range(n)
+    }
 
     @pl.when(w < m - 1)
     def _():
-        for copy in folds:
-            copy.start()
-
-    scatters = [remote(at(acc, j), rs.at[i], rs_s.at[k], rs_r.at[i], "lm", j) for k, j in enumerate(others)]
-    for k, j in enumerate(order):
-        spot = pl.ds(j * sh, sh)
+        for k in range(n - 1, -1, -1):
+            folds[k].start()
+
+    sends = []
+    for k in range(n - 1, -1, -1):
+        spot = pl.ds(peers[k] * sh, sh)
 
         @pl.when(w > 0)
         def _():
@@ -216,28 +227,70 @@
         def _():
             acc[spot] = h[spot]
 
-        if k < n - 1:
-            scatters[k].start()
-    total = acc[pl.ds(i * sh, sh)]
-    arrive = [lax.rem(i + n - k, n) for k in range(1, n)]
-    for j in arrive:
-        remote(at(acc, j), rs.at[j], rs_s.at[0], rs_r.at[j], "lm", j).wait_recv()
-        total = total + rs[j]
-    full[pl.ds(i * sh, sh)] = total
-    gathers = [remote(at(full, i), at(full, i), ag_s.at[k], ag_r.at[i], "lm", j) for k, j in enumerate(others)]
-    for copy in gathers:
+        if k > 0:
+            copy = remote(at(acc, peers[k]), rs.at[k], rs_s.at[k], rs_r.at[k], "lm", peers[k])
+            copy.start()
+            sends.append(copy)
+    here = pl.ds(i * sh, sh)
+    total = acc[here]
+    for k in range(1, n):
+        remote(at(acc, i), rs.at[k], rs_s.at[k], rs_r.at[k], "lm", peers[k]).wait_recv()
+        total = total + rs[k]
+    value, products = on_shard(here, total)
+    full[here] = value
+    if products:
+        rows = lax.broadcasted_iota(jnp.int32, near.shape[1:], 0)
+        tile = jnp.zeros(near.shape[1:], jnp.float32)
+        for r, product in enumerate(products):
+            tile = jnp.where(rows == r, jnp.sum(jnp.sum(product, axis=0), axis=0, keepdims=True), tile)
+        near[i] = tile
+        for k in outward:
+            copy = remote(near.at[i], near.at[i], near_s.at[k], near_r.at[k], "lm", peers[k])
+            copy.start()
+            sends.append(copy)
+    for k in outward:
+        copy = remote(at(full, i), at(full, i), ag_s.at[k], ag_r.at[k], "lm", peers[k])
         copy.start()
-    forwards = []
-    for k, j in enumerate([i] + arrive):
+        sends.append(copy)
+    forwards = [
+        remote(at(full, peers[k]), at(full, peers[k], own), fw_s.at[k], fw_r.at[k], "kf", former)
+        for k in range(n if pair else 0)
+    ]
+
+    def collect(k):
         if k > 0:
-            remote(at(full, j), at(full, j), ag_s.at[0], ag_r.at[j], "lm", j).wait_recv()
+            remote(at(full, peers[k]), at(full, peers[k]), ag_s.at[k], ag_r.at[k], "lm", peers[k]).wait_recv()
         if pair:
-            copy = remote(at(full, j), at(full, j, own), fw_s.at[k], fw_r.at[k], "kf", former)
-            forwards.append(copy)
 
             @pl.when(w > 0)
             def _():
-                copy.start()
+                forwards[k].start()
+
+    for k in range(n // 2):
+        collect(k)
+    if products:
+        for k in range(1, n):
+            remote(near.at[i], near.at[peers[k]], near_s.at[k], near_r.at[k], "lm", peers[k]).wait_recv()
+        tile = near[0]
+        for j in range(1, n):
+            tile = tile + near[j]
+        far[w] = tile
+        for k in range(1, m):
+            copy = remote(far.at[w], far.at[w], far_s.at[k], far_r.at[w], "kf", lax.rem(w + k, m))
+            copy.start()
+            sends.append(copy)
+    for k in range(n // 2, n):
+        collect(k)
+
+    def sums():
+        for k in range(1, m):
+            j = lax.rem(w + k, m)
+            remote(far.at[j], far.at[j], far_s.at[k], far_r.at[j], "kf", j).wait_recv()
+        tile = far[0]
+        for j in range(1, m):
+            tile = tile + far[j]
+        tile = jnp.sum(tile, axis=1, keepdims=True)
+        return [tile[r:r + 1] for r in range(len(products))]
 
     def finish_pair():
         @pl.when(w < m - 1)
@@ -252,10 +305,10 @@
     def finish_sends():
         @pl.when(w < m - 1)
         def _():
-            for copy in folds:
-                copy.wait_send()
-
-        for copy in scatters + gathers:
+            for k in range(n):
+                folds[k].wait_send()
+
+        for copy in sends:
             copy.wait_send()
         if pair:
 
@@ -264,111 +317,115 @@
                 for copy in forwards:
                     copy.wait_send()
 
-    return finish_pair, finish_sends
-
-
-def over_windows(m, value, slots, send, recv):
-    w = lax.axis_index("kf")
-    slots[w] = jnp.sum(value, axis=0)
-    copies = []
-    for k in range(1, m):
-        copy = remote(slots.at[w], slots.at[w], send.at[k], recv.at[w], "kf", lax.rem(w + k, m))
-        copy.start()
-        copies.append(copy)
-    for k in range(1, m):
-        j = lax.rem(w + k, m)
-        remote(slots.at[j], slots.at[j], send.at[0], recv.at[j], "kf", j).wait_recv()
-    total = slots[0]
-    for j in range(1, m):
-        total = total + slots[j]
-
-    def finish():
-        for copy in copies:
-            copy.wait_send()
-
-    return jnp.sum(jnp.sum(total, axis=0, keepdims=True), axis=1, keepdims=True), finish
+    return sums, finish_pair, finish_sends
 
 
 def columns(g):
     return pl.ds(g * LANES, LANES)
 
 
-def first_phase(n, m, h, damping, jacobi_scale, res_out, dir_out, energy_out, diag_out, full, fold, acc, rs, slots, diag, *sems):
+def first_phase(n, m, h, damping, jacobi_scale, res_out, dir_out, scale_out, damp_out, full, fold, acc, rs, near, far, *sems):
     own = acc.shape[0]
+    sh = own // n
     state = damping.shape[0]
-    w = lax.axis_index("kf")
-    diag[...] = jnp.zeros_like(diag)
+    i, w = lax.axis_index("lm"), lax.axis_index("kf")
+    here, upper = pl.ds(0, own), pl.ds(own, own)
+    met = greet(n, m)
+    scale, scale_sems = sems[-2], sems[-1]
+    rest = pl.ds(state, PAD - state)
+    scale[here, rest, :] = jnp.zeros((own, PAD - state, LANES), jnp.float32)
     for g in range(own):
-        diag[g, pl.ds(0, state), :] = damping[:, columns(g)]
-        diag[g, pl.ds(PAD, state), :] = jacobi_scale[:, columns(g)]
-    greet(n, m)
-    diag_copy = remote(
-        diag.at[pl.ds(0, own)], diag.at[pl.ds(own, own)], sems[10].at[0], sems[10].at[1], "kf", lax.rem(w + m - 1, m)
+        scale[g, pl.ds(0, state), :] = jacobi_scale[:, columns(g)]
+    damp_out[:, rest, :] = jnp.zeros((sh, PAD - state, LANES), jnp.float32)
+    for g in range(sh):
+        spot = pl.ds(pl.multiple_of((i * sh + g) * LANES, LANES), LANES)
+        damp_out[g, pl.ds(0, state), :] = damping[:, spot]
+    met()
+    scale_copy = remote(
+        scale.at[here], scale.at[upper], scale_sems.at[0], scale_sems.at[1], "kf", lax.rem(w + m - 1, m)
     )
 
     @pl.when(w > 0)
     def _():
-        diag_copy.start()
-
-    finish_pair, finish_sends = reduce_spread(n, m, True, h, full, (fold, acc, rs), sems[:8])
-    grad = full[pl.ds(0, own)]
-    scale = diag[pl.ds(0, own), pl.ds(PAD, PAD), :]
-    energy, finish = over_windows(m, grad * grad * scale, slots.at[0], sems[8].at[0], sems[9].at[0])
-    energy_out[...] = jnp.broadcast_to(energy, energy_out.shape)
-    finish_pair()
+        scale_copy.start()
+
+    _, finish_pair, finish_sends = all_reduce(
+        n, m, True, h, full, (fold, acc, rs, near, far), sems[:-2], lambda here, total: (-total, ())
+    )
+
+    res_out[here] = full[here]
+    dir_out[here] = full[here] * scale[here]
+    scale_out[here] = scale[here]
 
     @pl.when(w < m - 1)
     def _():
-        diag_copy.wait_recv()
+        scale_copy.wait_recv()
+
+    @pl.when(w == m - 1)
+    def _():
+        scale[upper] = jnp.zeros((own,) + scale.shape[1:], jnp.float32)
+
+    finish_pair()
+    res_out[upper] = full[upper]
+    dir_out[upper] = full[upper] * scale[upper]
+    scale_out[upper] = scale[upper]
 
     @pl.when(w > 0)
     def _():
-        diag_copy.wait_send()
-
-    res_out[...] = -full[...]
-    dir_out[...] = -full[...] * diag[:, pl.ds(PAD, PAD), :]
-    diag_out[...] = diag[...]
-    finish()
+        scale_copy.wait_send()
+
     finish_sends()
 
 
-def middle_phase(begun, n, m, h, res, direction, diag, energy_in, *rest):
+def middle_phase(begun, n, m, h, res, direction, scale, damp, *rest):
     if begun:
         answer_in, *rest = rest
-    res_out, dir_out, energy_out, answer_out, full, fold, acc, rs, slots, *sems = rest
+    res_out, dir_out, answer_out, full, fold, acc, rs, near, far, *sems = rest
     own = acc.shape[0]
-    here, damp, scale = pl.ds(0, own), pl.ds(0, PAD), pl.ds(PAD, PAD)
-    greet(n, m)
-    finish_pair, finish_sends = reduce_spread(n, m, True, h, full, (fold, acc, rs), sems[:8])
-    energy = energy_in[pl.ds(0, 1), pl.ds(0, 1)]
-    applied = full[here] + diag[here, damp, :] * direction[here]
-    curve, finish_a = over_windows(m, direction[here] * applied, slots.at[0], sems[8].at[0], sems[9].at[0])
+    here = pl.ds(0, own)
+    greet(n, m)()
+
+    def on_shard(here, total):
+        along, left, scaled = direction[here], res[here], scale[here]
+        applied = total + damp[...] * along
+        scaled_applied, scaled_left = scaled * applied, scaled * left
+        return applied, (along * applied, left * scaled_applied, applied * scaled_applied, left * scaled_left)
+
+    sums, finish_pair, finish_sends = all_reduce(
+        n, m, True, h, full, (fold, acc, rs, near, far), sems, on_shard
+    )
+    curve, cross, square, energy = sums()
     step = energy / curve
-    after = res[here] - step * applied
-    fresh, finish_b = over_windows(m, after * after * diag[here, scale, :], slots.at[1], sems[8].at[1], sems[9].at[1])
+    ratio = (energy - 2.0 * step * cross + step * step * square) / energy
+
+    def advance(part):
+        after = res[part] - step * full[part]
+        res_out[part] = after
+        dir_out[part] = scale[part] * after + ratio * direction[part]
+
     gained = step * direction[here]
     answer_out[...] = answer_in[...] + gained if begun else gained
-    energy_out[...] = jnp.broadcast_to(fresh, energy_out.shape)
+    advance(here)
     finish_pair()
-    after = res[...] - step * (full[...] + diag[:, damp, :] * direction[...])
-    res_out[...] = after
-    dir_out[...] = diag[:, scale, :] * after + fresh / energy * direction[...]
-    finish_a()
-    finish_b()
+    advance(pl.ds(own, own))
     finish_sends()
 
 
-def last_phase(n, m, h, direction, diag, energy_in, applied_out, step_out, full, fold, acc, rs, slots, *sems):
+def last_phase(n, m, h, res, direction, scale, damp, applied_out, step_out, full, fold, acc, rs, near, far, *sems):
     own = acc.shape[0]
-    here = pl.ds(0, own)
-    greet(n, m)
-    _, finish_sends = reduce_spread(n, m, False, h, full, (fold, acc, rs), sems[:8])
-    applied = full[here] + diag[here, pl.ds(0, PAD), :] * direction[here]
-    applied_out[...] = applied
-    curve, finish = over_windows(m, direction[here] * applied, slots.at[0], sems[8].at[0], sems[9].at[0])
-    step = energy_in[pl.ds(0, 1), pl.ds(0, 1)] / curve
-    step_out[...] = jnp.broadcast_to(step, step_out.shape)
-    finish()
+    greet(n, m)()
+
+    def on_shard(here, total):
+        along, left = direction[here], res[here]
+        applied = total + damp[...] * along
+        return applied, (along * applied, left * left * scale[here])
+
+    sums, _, finish_sends = all_reduce(
+        n, m, False, h, full, (fold, acc, rs, near, far), sems, on_shard
+    )
+    curve, energy = sums()
+    step_out[...] = jnp.broadcast_to(energy / curve, step_out.shape)
+    applied_out[...] = full[pl.ds(0, own)]
     finish_sends()
 
 
@@ -411,12 +468,12 @@
             pltpu.VMEM((own,) + tile, jnp.float32),
             pltpu.VMEM((own,) + tile, jnp.float32),
             pltpu.VMEM((n, own // n) + tile, jnp.float32),
-            pltpu.VMEM((2, m) + tile, jnp.float32),
+            pltpu.VMEM((n, 8, LANES), jnp.float32),
+            pltpu.VMEM((m, 8, LANES), jnp.float32),
         ]
-        + [pltpu.VMEM(shape, jnp.float32) for shape in extra]
-        + [dma((n,))] * 8
-        + [dma((2, m))] * 2
-        + [dma((2,))],
+        + [dma((n,))] * 10
+        + [dma((m,))] * 2
+        + extra,
         compiler_params=pltpu.CompilerParams(collective_id=number, has_side_effects=True, vmem_limit_bytes=LIMIT),
         name=name,
     )(*operands)
@@ -429,7 +486,6 @@
     starts = jnp.minimum((frame_ids[:, 0] - lax.axis_index("kf") * frames) >> 7, 2 * own - SPAN)
     n, m = lax.axis_size("lm"), lax.axis_size("kf")
     pair, one, tile = (2 * own, PAD, LANES), (own, PAD, LANES), (8, LANES)
-    both = (2 * own, 2 * PAD, LANES)
     vmem = pl.BlockSpec(memory_space=pltpu.VMEM)
     gradient, code, inverse, jac, null = local_call(
         gradient_kernel, "local_gradient",
@@ -453,17 +509,18 @@
             starts, field, code, inverse, jac, null,
         )[0]
 
-    residual, direction, energy, diag = phase(
-        first_phase, "first_phase", 0, n, m, (pair, pair, tile, both), (both,), gradient, damping, jacobi_scale
+    residual, direction, scale, damp = phase(
+        first_phase, "first_phase", 0, n, m, (pair, pair, pair, (own // n, PAD, LANES)),
+        [pltpu.VMEM(pair, jnp.float32), pltpu.SemaphoreType.DMA((2,))], gradient, damping, jacobi_scale,
     )
     answer = ()
     for number in range(1, ITERS):
-        residual, direction, energy, *answer = phase(
-            functools.partial(middle_phase, number > 1), "middle_phase", number, n, m, (pair, pair, tile, one), (),
-            product(direction), residual, direction, diag, energy, *answer,
+        residual, direction, *answer = phase(
+            functools.partial(middle_phase, number > 1), "middle_phase", number, n, m, (pair, pair, one), [],
+            product(direction), residual, direction, scale, damp, *answer,
         )
     applied, step = phase(
-        last_phase, "last_phase", ITERS, n, m, (one, tile), (), product(direction), direction, diag, energy
+        last_phase, "last_phase", ITERS, n, m, (one, tile), [], product(direction), residual, direction, scale, damp
     )
     return tuple(last_update(damping.shape, residual, direction, applied, *answer, step))
 

time: 108 us -> 101 us (0.935)
  Pallas kernels: 101 us -> 93.7 us
    pallas_call x3, Pallas kernels: 74.3 us -> 67.2 us  [phase(): pl.pallas_call(functools.partial(kernel, n, m), in_specs=[vmem] * len(ope...]
where the time goes in v2:
time: 101 us; the launch traced here: 100 us
  Pallas kernels  93.7 us (93%)
  local copies, waits for them, and re-layouts  5.39 us (5%)
    pallas_call x3, Pallas kernels, phase(): pl.pallas_call(functools.partial(kernel, n, m), in_specs=[vmem] * len(ope...  67.2 us
    pallas_call x3, Pallas kernels, local_call(): pl.pallas_call(kernel, in_specs=[pl.BlockSpec(memory_space=pltpu.SMEM)] +...  25.6 us
    unnamed x14, local copies, waits for them, and re-layouts  5.39 us

profile of v2, /device:TPU:0, one launch (start us, length us, event | category | flops | bytes accessed | tf_op | source)
XLA Modules:
  0.0 100.5 jit_solution(7158200548694765218)
XLA Ops:
  0.6 0.7 minimum_bitcast_fusion.starts
  1.3 0.0 copy-start
  1.3 2.2 %copy-done = bf16[128,128,128]{2,1,0:T(8,128)(2,1)S(1)} copy-done((bf16[128,128,128]{2,1,0:T(8,128)(2,1)S(1)}, bf16[128,128,128]{2,1,0:T(8,128)(2,1)}, u32[]{:S(2)}) %copy-start) | copy-done | bytes 4194328
  3.5 0.0 copy-start.1
  3.5 1.0 %copy-done.1 = bf16[128,15,128]{2,0,1:T(8,128)(2,1)S(1)} copy-done((bf16[128,15,128]{2,0,1:T(8,128)(2,1)S(1)}, bf16[128,15,128]{2,0,1:T(8,128)(2,1)}, u32[]{:S(2)}) %copy-start.1) | copy-done | bytes 491544
  4.5 0.0 copy-start.4
  4.5 0.8 copy-done.4
  5.3 0.0 copy-start.5
  5.3 0.8 copy-done.5
  6.1 0.0 copy-start.6
  6.1 0.7 copy-done.6
  6.7 0.0 copy-start.2
  6.7 0.0 copy-start.3
  6.7 9.6 %local_gradient.1 = (f32[64,16,128]{2,1,0:T(8,128)S(1)}, s32[128,128]{1,0:T(8,128)S(1)}, s32[128,8,128]{2,1,0:T(8,128)S(1)}, f32[2048,128]{1,0:T(8,128)S(1)}, bf16[128,128,128]{2,1,0:T(8,128)(2,1)S(1)}) custom-call(s32[128]{0:T(128)S(1)} %minimum_bitcast_fusion.starts, s32[64,128]{1,0:T(8,128)S(1)} %bitcast.9, s32[1,128]{1,0:T(1,128)S(1)} %bitcast.10, ...), custom_call_target="tpu_custom_call" | custom-call | tf_op jit(solution)/shard_map/local_gradient/pallas_call | solution.py:154
  16.3 0.0 copy-done.2
  16.3 0.0 copy-done.3
  16.3 21.7 %first_phase.1 = (f32[64,16,128]{2,1,0:T(8,128)S(1)}, f32[64,16,128]{2,1,0:T(8,128)S(1)}, f32[64,16,128]{2,1,0:T(8,128)S(1)}, f32[4,16,128]{2,1,0:T(8,128)S(1)}) custom-call(f32[64,16,128]{2,1,0:T(8,128)S(1)} %get-tuple-element.16.h, f32[15,4096]{1,0:T(8,128)S(1)} %copy-done.2, f32[15,4096]{1,0:T(8,128)S(1)} %copy-done.3), custom_call_target="tpu_custom_call" | custom-call | tf_op jit(solution)/shard_map/first_phase/pallas_call | solution.py:461
  38.0 8.0 %local_field.2.h = f32[64,16,128]{2,1,0:T(8,128)S(1)} custom-call(s32[128]{0:T(128)S(1)} %minimum_bitcast_fusion.starts, f32[64,16,128]{2,1,0:T(8,128)S(1)} %get-tuple-element.17.field_ref.direction, s32[128,128]{1,0:T(8,128)S(1)} %get-tuple-element.18.code_ref, s32[128,8,128]{2,1,0:T(8,128)S(1)} %get-tuple-element.19.inv_ref, f32[128,16,128]{2,1,0:T(8,128)S(1)} %bitcast.6, ...), custom_call_target="tpu_custom_call" | custom-call | tf_op jit(solution)/shard_map/local_field/pallas_call | solution.py:154
  46.0 24.4 %middle_phase.1 = (f32[64,16,128]{2,1,0:T(8,128)S(1)}, f32[64,16,128]{2,1,0:T(8,128)S(1)}, f32[32,16,128]{2,1,0:T(8,128)S(1)}) custom-call(f32[64,16,128]{2,1,0:T(8,128)S(1)} %local_field.2.h, f32[64,16,128]{2,1,0:T(8,128)S(1)} %get-tuple-element.22.res, f32[64,16,128]{2,1,0:T(8,128)S(1)} %get-tuple-element.17.field_ref.direction, ...), custom_call_target="tpu_custom_call" | custom-call | tf_op jit(solution)/shard_map/middle_phase/pallas_call | solution.py:461
  70.4 8.0 %local_field.3.h = f32[64,16,128]{2,1,0:T(8,128)S(1)} custom-call(s32[128]{0:T(128)S(1)} %minimum_bitcast_fusion.starts, f32[64,16,128]{2,1,0:T(8,128)S(1)} %get-tuple-element.26.field_ref.direction, s32[128,128]{1,0:T(8,128)S(1)} %get-tuple-element.18.code_ref, s32[128,8,128]{2,1,0:T(8,128)S(1)} %get-tuple-element.19.inv_ref, f32[128,16,128]{2,1,0:T(8,128)S(1)} %bitcast.7, ...), custom_call_target="tpu_custom_call" | custom-call | tf_op jit(solution)/shard_map/local_field/pallas_call | solution.py:154
  78.4 21.2 %last_phase.1 = (f32[32,16,128]{2,1,0:T(8,128)S(1)}, f32[8,128]{1,0:T(8,128)S(1)}) custom-call(f32[64,16,128]{2,1,0:T(8,128)S(1)} %local_field.3.h, f32[64,16,128]{2,1,0:T(8,128)S(1)} %get-tuple-element.25.res, f32[64,16,128]{2,1,0:T(8,128)S(1)} %get-tuple-element.26.field_ref.direction, f32[64,16,128]{2,1,0:T(8,128)S(1)} %get-tuple-element.23.scale, ...), custom_call_target="tpu_custom_call" | custom-call | tf_op jit(solution)/shard_map/last_phase/pallas_call | solution.py:461
  99.6 0.9 last_update.1
Async XLA Ops:
  1.3 2.2 %copy-start = (bf16[128,128,128]{2,1,0:T(8,128)(2,1)S(1)}, bf16[128,128,128]{2,1,0:T(8,128)(2,1)}, u32[]{:S(2)}) copy-start(bf16[128,128,128]{2,1,0:T(8,128)(2,1)} %null_in.1) | copy-start | bytes 12582916
  3.5 1.0 %copy-start.1 = (bf16[128,15,128]{2,0,1:T(8,128)(2,1)S(1)}, bf16[128,15,128]{2,0,1:T(8,128)(2,1)}, u32[]{:S(2)}) copy-start(bf16[128,15,128]{2,0,1:T(8,128)(2,1)} %param.8) | copy-start | bytes 1474564
  4.5 0.8 copy-start.4
  5.3 0.8 copy-start.5
  6.1 0.7 copy-start.6
  6.7 9.6 %copy-start.2 = (f32[15,4096]{1,0:T(8,128)S(1)}, f32[15,4096]{1,0:T(8,128)}, u32[]{:S(2)}) copy-start(f32[15,4096]{1,0:T(8,128)} %damping.1) | copy-start | bytes 737284
  6.7 9.6 %copy-start.3 = (f32[15,4096]{1,0:T(8,128)S(1)}, f32[15,4096]{1,0:T(8,128)}, u32[]{:S(2)}) copy-start(f32[15,4096]{1,0:T(8,128)} %jacobi_scale.1) | copy-start | bytes 737284

commit v3 on v2

--- a/solution.py
+++ b/solution.py
@@ -92,23 +92,13 @@
 
 
 def gradient_kernel(
-    starts, ids_ref, count_ref, rows_ref, jac_in, null_in,
-    out_ref, code_ref, inv_ref, jac_ref, null_ref, row_ref, slot_ref, sems,
+    starts, offs_ref, rows_ref, jac_in, null_ref, out_ref, code_ref, inv_ref, jac_ref, row_ref, slot_ref
 ):
     blocks = null_ref.shape[0]
     chunks = blocks // CHUNK
-    copies = []
-    for c in range(chunks):
-        mine = pl.ds(c * CHUNK, CHUNK)
-        copies.append(pltpu.make_async_copy(null_in.at[mine], null_ref.at[mine], sems.at[c]))
-        copies[c].start()
     out_ref[...] = jnp.zeros_like(out_ref)
-    frames = out_ref.shape[0] // 2 * LANES
-    ids = ids_ref[...] - lax.axis_index("kf") * frames
-    begin = jnp.minimum(ids[:1] >> 7, out_ref.shape[0] - SPAN)
-    slots = lax.broadcasted_iota(jnp.int32, ids.shape, 0)
-    ids = jnp.where(slots < count_ref[...], ids - begin * LANES, DEAD)
-    offs = jnp.transpose(jnp.concatenate([ids] * (LANES // ids.shape[0]), axis=0))
+    offs = offs_ref[...]
+    offs = jnp.transpose(jnp.concatenate([offs] * (LANES // offs.shape[0]), axis=0))
     slot_ref[...] = offs
     lanes = lax.broadcasted_iota(jnp.int32, offs.shape, 1)
     code_ref[...] = along_lanes(offs, lanes >> 1)
@@ -123,9 +113,6 @@
     even = even_lanes()
     tile = (PICK, LANES)
     target = lax.broadcasted_iota(jnp.int32, tile, 0) * LANES + lax.broadcasted_iota(jnp.int32, tile, 1)
-    for c in range(chunks):
-        copies[c].wait()
-
     @pl.loop(0, chunks)
     def _(step):
         base = pl.multiple_of(step * CHUNK, CHUNK)
@@ -140,7 +127,7 @@
         for i in range(CHUNK):
             offset = jnp.broadcast_to(offsets[pl.ds(i, 1), :], tile)
             at = jnp.zeros(tile, jnp.int32)
-            width = ids_ref.shape[0] // 2
+            width = offs_ref.shape[0] // 2
             while width > 0:
                 at = jnp.where(along_lanes(offset, at + width) <= target, at + width, at)
                 width //= 2
@@ -163,9 +150,10 @@
 
 
 def remote(src, dst, send, recv, axis, index):
+    where = dict(zip(axis, index)) if isinstance(axis, tuple) else {axis: index}
     return pltpu.make_async_remote_copy(
         src_ref=src, dst_ref=dst, send_sem=send, recv_sem=recv,
-        device_id={axis: index}, device_id_type=pl.DeviceIdType.MESH,
+        device_id=where, device_id_type=pl.DeviceIdType.MESH,
     )
 
 
@@ -181,21 +169,26 @@
 def greet(n, m):
     i, w = lax.axis_index("lm"), lax.axis_index("kf")
     barrier = pltpu.get_barrier_semaphore()
-    for k in range(n - 1, 0, -1):
-        pl.semaphore_signal(
-            barrier, inc=1, device_id={"lm": partner(i, k)}, device_id_type=pl.DeviceIdType.MESH
-        )
-    for k in range(1, m):
-        pl.semaphore_signal(
-            barrier, inc=1, device_id={"kf": lax.rem(w + k, m)}, device_id_type=pl.DeviceIdType.MESH
-        )
-    return lambda: pl.semaphore_wait(barrier, n - 1 + m - 1)
+    count = 0
+
+    def signal(j, v):
+        pl.semaphore_signal(barrier, inc=1, device_id={"lm": j, "kf": v}, device_id_type=pl.DeviceIdType.MESH)
+        return 1
+
+    for k in range(n - 1, -1, -1):
+        for step in (1, m - 1):
+            count += signal(partner(i, k), lax.rem(w + step, m))
+        if k > 0:
+            count += signal(partner(i, k), w)
+    for step in range(2, m - 1):
+        count += signal(i, lax.rem(w + step, m))
+    return lambda: pl.semaphore_wait(barrier, count)
 
 
 def all_reduce(n, m, pair, h, full, bufs, sems, on_shard):
-    fold, acc, rs, near, far = bufs
-    fold_s, fold_r, rs_s, rs_r, ag_s, ag_r, fw_s, fw_r, near_s, near_r, far_s, far_r = sems
-    own = acc.shape[0]
+    acc, rs, near, far = bufs
+    up_s, up_r, rs_s, rs_r, ag_s, ag_r, fw_s, fw_r, near_s, near_r, far_s, far_r = sems
+    own = h.shape[0] // 2
     sh = own // n
     i, w = lax.axis_index("lm"), lax.axis_index("kf")
     later, former = lax.rem(w + 1, m), lax.rem(w + m - 1, m)
@@ -205,37 +198,38 @@
 
     peers = [partner(i, k) for k in range(n)]
     outward = range(n - 1, 0, -1)
-    folds = {
-        k: remote(at(h, peers[k], own), at(fold, peers[k]), fold_s.at[k], fold_r.at[k], "kf", later) for k in range(n)
-    }
-
-    @pl.when(w < m - 1)
+    uppers = [
+        remote(at(h, peers[k], own), rs.at[n + k], up_s.at[k], up_r.at[k], ("lm", "kf"), (peers[k], later))
+        for k in range(n)
+    ]
+    lowers = [
+        remote(at(h, peers[k]), rs.at[k], rs_s.at[k], rs_r.at[k], "lm", peers[k]) for k in outward
+    ]
+    for k in range(n - 1, -1, -1):
+
+        @pl.when(w < m - 1)
+        def _():
+            uppers[k].start()
+
+        if k > 0:
+            lowers[n - 1 - k].start()
+    sends = list(lowers)
+    here = pl.ds(i * sh, sh)
+    total = h[here]
+    for copy, k in zip(lowers[::-1], range(1, n)):
+        copy.wait_recv()
+        total = total + rs[k]
+    acc[...] = total
+
+    @pl.when(w > 0)
     def _():
-        for k in range(n - 1, -1, -1):
-            folds[k].start()
-
-    sends = []
-    for k in range(n - 1, -1, -1):
-        spot = pl.ds(peers[k] * sh, sh)
-
-        @pl.when(w > 0)
-        def _():
-            folds[k].wait_recv()
-            acc[spot] = h[spot] + fold[spot]
-
-        @pl.when(w == 0)
-        def _():
-            acc[spot] = h[spot]
-
-        if k > 0:
-            copy = remote(at(acc, peers[k]), rs.at[k], rs_s.at[k], rs_r.at[k], "lm", peers[k])
-            copy.start()
-            sends.append(copy)
-    here = pl.ds(i * sh, sh)
-    total = acc[here]
-    for k in range(1, n):
-        remote(at(acc, i), rs.at[k], rs_s.at[k], rs_r.at[k], "lm", peers[k]).wait_recv()
-        total = total + rs[k]
+        more = acc[...]
+        for k in range(n):
+            uppers[k].wait_recv()
+            more = more + rs[n + k]
+        acc[...] = more
+
+    total = acc[...]
     value, products = on_shard(here, total)
     full[here] = value
     if products:
@@ -306,7 +300,7 @@
         @pl.when(w < m - 1)
         def _():
             for k in range(n):
-                folds[k].wait_send()
+                uppers[k].wait_send()
 
         for copy in sends:
             copy.wait_send()
@@ -324,8 +318,8 @@
     return pl.ds(g * LANES, LANES)
 
 
-def first_phase(n, m, h, damping, jacobi_scale, res_out, dir_out, scale_out, damp_out, full, fold, acc, rs, near, far, *sems):
-    own = acc.shape[0]
+def first_phase(n, m, h, damping, jacobi_scale, res_out, dir_out, scale_out, damp_out, full, acc, rs, near, far, *sems):
+    own = full.shape[0] // 2
     sh = own // n
     state = damping.shape[0]
     i, w = lax.axis_index("lm"), lax.axis_index("kf")
@@ -350,7 +344,7 @@
         scale_copy.start()
 
     _, finish_pair, finish_sends = all_reduce(
-        n, m, True, h, full, (fold, acc, rs, near, far), sems[:-2], lambda here, total: (-total, ())
+        n, m, True, h, full, (acc, rs, near, far), sems[:-2], lambda here, total: (-total, ())
     )
 
     res_out[here] = full[here]
@@ -380,8 +374,8 @@
 def middle_phase(begun, n, m, h, res, direction, scale, damp, *rest):
     if begun:
         answer_in, *rest = rest
-    res_out, dir_out, answer_out, full, fold, acc, rs, near, far, *sems = rest
-    own = acc.shape[0]
+    res_out, dir_out, answer_out, full, acc, rs, near, far, *sems = rest
+    own = full.shape[0] // 2
     here = pl.ds(0, own)
     greet(n, m)()
 
@@ -392,7 +386,7 @@
         return applied, (along * applied, left * scaled_applied, applied * scaled_applied, left * scaled_left)
 
     sums, finish_pair, finish_sends = all_reduce(
-        n, m, True, h, full, (fold, acc, rs, near, far), sems, on_shard
+        n, m, True, h, full, (acc, rs, near, far), sems, on_shard
     )
     curve, cross, square, energy = sums()
     step = energy / curve
@@ -411,8 +405,8 @@
     finish_sends()
 
 
-def last_phase(n, m, h, res, direction, scale, damp, applied_out, step_out, full, fold, acc, rs, near, far, *sems):
-    own = acc.shape[0]
+def last_phase(n, m, h, res, direction, scale, damp, applied_out, step_out, full, acc, rs, near, far, *sems):
+    own = full.shape[0] // 2
     greet(n, m)()
 
     def on_shard(here, total):
@@ -421,7 +415,7 @@
         return applied, (along * applied, left * left * scale[here])
 
     sums, _, finish_sends = all_reduce(
-        n, m, False, h, full, (fold, acc, rs, near, far), sems, on_shard
+        n, m, False, h, full, (acc, rs, near, far), sems, on_shard
     )
     curve, energy = sums()
     step_out[...] = jnp.broadcast_to(energy / curve, step_out.shape)
@@ -465,9 +459,8 @@
         out_shape=[jax.ShapeDtypeStruct(shape, jnp.float32) for shape in outs],
         scratch_shapes=[
             pltpu.VMEM(pair, jnp.float32),
-            pltpu.VMEM((own,) + tile, jnp.float32),
-            pltpu.VMEM((own,) + tile, jnp.float32),
-            pltpu.VMEM((n, own // n) + tile, jnp.float32),
+            pltpu.VMEM((own // n,) + tile, jnp.float32),
+            pltpu.VMEM((2 * n, own // n) + tile, jnp.float32),
             pltpu.VMEM((n, 8, LANES), jnp.float32),
             pltpu.VMEM((m, 8, LANES), jnp.float32),
         ]
@@ -483,30 +476,30 @@
     state, frames = damping.shape
     own = frames // LANES
     blocks = nullspace.shape[0]
-    starts = jnp.minimum((frame_ids[:, 0] - lax.axis_index("kf") * frames) >> 7, 2 * own - SPAN)
+    ids = jnp.transpose(frame_ids) - lax.axis_index("kf") * frames
+    starts = jnp.minimum(ids[0] >> 7, 2 * own - SPAN)
+    slots = lax.broadcasted_iota(jnp.int32, ids.shape, 0)
+    offsets = jnp.where(slots < obs_count[None, :], ids - starts[None, :] * LANES, DEAD)
     n, m = lax.axis_size("lm"), lax.axis_size("kf")
     pair, one, tile = (2 * own, PAD, LANES), (own, PAD, LANES), (8, LANES)
     vmem = pl.BlockSpec(memory_space=pltpu.VMEM)
-    gradient, code, inverse, jac, null = local_call(
+    gradient, code, inverse, jac = local_call(
         gradient_kernel, "local_gradient",
         [
             jax.ShapeDtypeStruct(pair, jnp.float32),
             jax.ShapeDtypeStruct((blocks, LANES), jnp.int32),
             jax.ShapeDtypeStruct((blocks, PICK, LANES), jnp.int32),
             jax.ShapeDtypeStruct((blocks * PAD, LANES), jnp.float32),
-            jax.ShapeDtypeStruct(nullspace.shape, nullspace.dtype),
         ],
-        [pltpu.VMEM((blocks, LANES), jnp.int32), pltpu.SemaphoreType.DMA((blocks // CHUNK,))],
-        [vmem] * 4 + [pl.BlockSpec(memory_space=pltpu.HBM)],
-        starts, jnp.transpose(frame_ids), obs_count[None, :], residual_rows,
-        jnp.transpose(jacobian, (1, 0, 2)), nullspace,
+        [pltpu.VMEM((blocks, LANES), jnp.int32)], [vmem] * 4,
+        starts, offsets, residual_rows, jnp.transpose(jacobian, (1, 0, 2)), nullspace,
     )
     jac = jac.reshape(blocks, PAD, LANES)
 
     def product(field):
         return local_call(
             product_kernel, "local_field", [jax.ShapeDtypeStruct(pair, jnp.float32)], [], [vmem] * 5,
-            starts, field, code, inverse, jac, null,
+            starts, field, code, inverse, jac, nullspace,
         )[0]
 
     residual, direction, scale, damp = phase(

time: 101 us -> 112 us (1.11); the launches traced: 100 us -> 110 us
  Pallas kernels: 93.7 us -> 104 us
  local copies, waits for them, and re-layouts: 5.39 us -> 3.98 us
    pallas_call x3, Pallas kernels: 67.2 us -> 77.8 us  [phase(): pl.pallas_call(functools.partial(kernel, n, m), in_specs=[vmem] * len(ope...]
    unnamed x14 -> x12, local copies, waits for them, and re-layouts: 5.39 us -> 3.98 us
where the time goes in v3:
time: 112 us; the launch traced here: 110 us
  Pallas kernels  104 us (93%)
  local copies, waits for them, and re-layouts  3.98 us (4%)
  other arithmetic  1.55 us (1%)
    pallas_call x3, Pallas kernels, phase(): pl.pallas_call(functools.partial(kernel, n, m), in_specs=[vmem] * len(ope...  77.8 us
    pallas_call x3, Pallas kernels, local_call(): pl.pallas_call(kernel, in_specs=[pl.BlockSpec(memory_space=pltpu.SMEM)] +...  25.3 us
    unnamed x12, local copies, waits for them, and re-layouts  3.98 us

profile of v3, /device:TPU:0, one launch (start us, length us, event | category | flops | bytes accessed | tf_op | source)
XLA Modules:
  0.0 110.2 jit_solution(11874843360602368756)
XLA Ops:
  0.6 0.8 subtract_bitcast_fusion
  1.4 0.8 subtract_select_fusion.offs_ref
  2.2 0.0 copy-start
  2.2 2.2 %copy-done = bf16[128,128,128]{2,1,0:T(8,128)(2,1)S(1)} copy-done((bf16[128,128,128]{2,1,0:T(8,128)(2,1)S(1)}, bf16[128,128,128]{2,1,0:T(8,128)(2,1)}, u32[]{:S(2)}) %copy-start) | copy-done | bytes 4194328
  4.4 0.0 copy-start.2
  4.4 1.0 copy-done.2
  5.4 0.0 copy-start.5
  5.4 0.8 copy-done.5
  6.2 0.0 copy-start.3
  6.2 0.0 copy-start.4
  6.2 0.0 copy-start.1
  6.2 9.3 %local_gradient.1 = (f32[64,16,128]{2,1,0:T(8,128)S(1)}, s32[128,128]{1,0:T(8,128)S(1)}, s32[128,8,128]{2,1,0:T(8,128)S(1)}, f32[2048,128]{1,0:T(8,128)S(1)}) custom-call(s32[128]{0:T(128)S(1)} %get-tuple-element.29.starts, s32[64,128]{1,0:T(8,128)S(1)} %subtract_select_fusion.offs_ref, bf16[128,128]{1,0:T(8,128)(2,1)S(1)} %copy-done.5, ...), custom_call_target="tpu_custom_call" | custom-call | tf_op jit(solution)/shard_map/local_gradient/pallas_call | solution.py:141
  15.4 0.0 copy-done.3
  15.4 0.0 copy-done.4
  15.5 26.2 %first_phase.1 = (f32[64,16,128]{2,1,0:T(8,128)S(1)}, f32[64,16,128]{2,1,0:T(8,128)S(1)}, f32[64,16,128]{2,1,0:T(8,128)S(1)}, f32[4,16,128]{2,1,0:T(8,128)S(1)}) custom-call(f32[64,16,128]{2,1,0:T(8,128)S(1)} %get-tuple-element.15.h, f32[15,4096]{1,0:T(8,128)S(1)} %copy-done.3, f32[15,4096]{1,0:T(8,128)S(1)} %copy-done.4), custom_call_target="tpu_custom_call" | custom-call | tf_op jit(solution)/shard_map/first_phase/pallas_call | solution.py:455
  41.7 0.0 copy-done.1
  41.7 8.0 %local_field.2.h = f32[64,16,128]{2,1,0:T(8,128)S(1)} custom-call(s32[128]{0:T(128)S(1)} %get-tuple-element.29.starts, f32[64,16,128]{2,1,0:T(8,128)S(1)} %get-tuple-element.16.field_ref.direction, s32[128,128]{1,0:T(8,128)S(1)} %get-tuple-element.17.code_ref, s32[128,8,128]{2,1,0:T(8,128)S(1)} %get-tuple-element.18.inv_ref, f32[128,16,128]{2,1,0:T(8,128)S(1)} %bitcast.10, ...), custom_call_target="tpu_custom_call" | custom-call | tf_op jit(solution)/shard_map/local_field/pallas_call | solution.py:141
  49.7 25.6 %middle_phase.1 = (f32[64,16,128]{2,1,0:T(8,128)S(1)}, f32[64,16,128]{2,1,0:T(8,128)S(1)}, f32[32,16,128]{2,1,0:T(8,128)S(1)}) custom-call(f32[64,16,128]{2,1,0:T(8,128)S(1)} %local_field.2.h, f32[64,16,128]{2,1,0:T(8,128)S(1)} %get-tuple-element.20.res, f32[64,16,128]{2,1,0:T(8,128)S(1)} %get-tuple-element.16.field_ref.direction, ...), custom_call_target="tpu_custom_call" | custom-call | tf_op jit(solution)/shard_map/middle_phase/pallas_call | solution.py:455
  75.4 8.0 %local_field.3.h = f32[64,16,128]{2,1,0:T(8,128)S(1)} custom-call(s32[128]{0:T(128)S(1)} %get-tuple-element.29.starts, f32[64,16,128]{2,1,0:T(8,128)S(1)} %get-tuple-element.24.field_ref.direction, s32[128,128]{1,0:T(8,128)S(1)} %get-tuple-element.17.code_ref, s32[128,8,128]{2,1,0:T(8,128)S(1)} %get-tuple-element.18.inv_ref, f32[128,16,128]{2,1,0:T(8,128)S(1)} %bitcast.11, ...), custom_call_target="tpu_custom_call" | custom-call | tf_op jit(solution)/shard_map/local_field/pallas_call | solution.py:141
  83.4 25.9 %last_phase.1 = (f32[32,16,128]{2,1,0:T(8,128)S(1)}, f32[8,128]{1,0:T(8,128)S(1)}) custom-call(f32[64,16,128]{2,1,0:T(8,128)S(1)} %local_field.3.h, f32[64,16,128]{2,1,0:T(8,128)S(1)} %get-tuple-element.23.res, f32[64,16,128]{2,1,0:T(8,128)S(1)} %get-tuple-element.24.field_ref.direction, f32[64,16,128]{2,1,0:T(8,128)S(1)} %get-tuple-element.21.scale, ...), custom_call_target="tpu_custom_call" | custom-call | tf_op jit(solution)/shard_map/last_phase/pallas_call | solution.py:455
  109.3 0.9 last_update.1
  (1 shorter events, 0.0 us)
Async XLA Ops:
  2.2 2.2 %copy-start = (bf16[128,128,128]{2,1,0:T(8,128)(2,1)S(1)}, bf16[128,128,128]{2,1,0:T(8,128)(2,1)}, u32[]{:S(2)}) copy-start(bf16[128,128,128]{2,1,0:T(8,128)(2,1)} %null_ref.5) | copy-start | bytes 12582916
  4.4 1.0 copy-start.2
  5.4 0.8 copy-start.5
  6.2 9.3 %copy-start.3 = (f32[15,4096]{1,0:T(8,128)S(1)}, f32[15,4096]{1,0:T(8,128)}, u32[]{:S(2)}) copy-start(f32[15,4096]{1,0:T(8,128)} %damping.1) | copy-start | bytes 737284
  6.2 9.3 %copy-start.4 = (f32[15,4096]{1,0:T(8,128)S(1)}, f32[15,4096]{1,0:T(8,128)}, u32[]{:S(2)}) copy-start(f32[15,4096]{1,0:T(8,128)} %jacobi_scale.1) | copy-start | bytes 737284
  6.2 35.5 %copy-start.1 = (bf16[128,128,128]{2,1,0:T(8,128)(2,1)S(1)}, bf16[128,128,128]{2,1,0:T(8,128)(2,1)}, u32[]{:S(2)}) copy-start(bf16[128,128,128]{2,1,0:T(8,128)(2,1)} %null_ref.5) | copy-start | bytes 12582916

commit v4 on v2

--- a/solution.py
+++ b/solution.py
@@ -50,7 +50,13 @@
 
 
 def along_lanes(tile, lanes):
-    return jnp.take_along_axis(tile, lanes, axis=1, mode="promise_in_bounds")
+    dims = lax.GatherDimensionNumbers(
+        offset_dims=(), collapsed_slice_dims=(1,), start_index_map=(1,),
+        operand_batching_dims=(0,), start_indices_batching_dims=(0,),
+    )
+    return lax.gather(
+        tile, lanes[..., None], dims, slice_sizes=(1, 1), mode=lax.GatherScatterMode.PROMISE_IN_BOUNDS
+    )
 
 
 def scatter_terms(starts, block, i, jac, row_ref, inv_ref, out_ref, even):
@@ -92,23 +98,13 @@
 
 
 def gradient_kernel(
-    starts, ids_ref, count_ref, rows_ref, jac_in, null_in,
-    out_ref, code_ref, inv_ref, jac_ref, null_ref, row_ref, slot_ref, sems,
+    starts, offs_ref, rows_ref, jac_in, null_ref, out_ref, code_ref, inv_ref, jac_ref, row_ref, slot_ref
 ):
     blocks = null_ref.shape[0]
     chunks = blocks // CHUNK
-    copies = []
-    for c in range(chunks):
-        mine = pl.ds(c * CHUNK, CHUNK)
-        copies.append(pltpu.make_async_copy(null_in.at[mine], null_ref.at[mine], sems.at[c]))
-        copies[c].start()
     out_ref[...] = jnp.zeros_like(out_ref)
-    frames = out_ref.shape[0] // 2 * LANES
-    ids = ids_ref[...] - lax.axis_index("kf") * frames
-    begin = jnp.minimum(ids[:1] >> 7, out_ref.shape[0] - SPAN)
-    slots = lax.broadcasted_iota(jnp.int32, ids.shape, 0)
-    ids = jnp.where(slots < count_ref[...], ids - begin * LANES, DEAD)
-    offs = jnp.transpose(jnp.concatenate([ids] * (LANES // ids.shape[0]), axis=0))
+    offs = offs_ref[...]
+    offs = jnp.transpose(jnp.concatenate([offs] * (LANES // offs.shape[0]), axis=0))
     slot_ref[...] = offs
     lanes = lax.broadcasted_iota(jnp.int32, offs.shape, 1)
     code_ref[...] = along_lanes(offs, lanes >> 1)
@@ -123,9 +119,6 @@
     even = even_lanes()
     tile = (PICK, LANES)
     target = lax.broadcasted_iota(jnp.int32, tile, 0) * LANES + lax.broadcasted_iota(jnp.int32, tile, 1)
-    for c in range(chunks):
-        copies[c].wait()
-
     @pl.loop(0, chunks)
     def _(step):
         base = pl.multiple_of(step * CHUNK, CHUNK)
@@ -140,7 +133,7 @@
         for i in range(CHUNK):
             offset = jnp.broadcast_to(offsets[pl.ds(i, 1), :], tile)
             at = jnp.zeros(tile, jnp.int32)
-            width = ids_ref.shape[0] // 2
+            width = offs_ref.shape[0] // 2
             while width > 0:
                 at = jnp.where(along_lanes(offset, at + width) <= target, at + width, at)
                 width //= 2
@@ -483,30 +476,30 @@
     state, frames = damping.shape
     own = frames // LANES
     blocks = nullspace.shape[0]
-    starts = jnp.minimum((frame_ids[:, 0] - lax.axis_index("kf") * frames) >> 7, 2 * own - SPAN)
+    ids = jnp.transpose(frame_ids) - lax.axis_index("kf") * frames
+    starts = jnp.minimum(ids[0] >> 7, 2 * own - SPAN)
+    slots = lax.broadcasted_iota(jnp.int32, ids.shape, 0)
+    offsets = jnp.where(slots < obs_count[None, :], ids - starts[None, :] * LANES, DEAD)
     n, m = lax.axis_size("lm"), lax.axis_size("kf")
     pair, one, tile = (2 * own, PAD, LANES), (own, PAD, LANES), (8, LANES)
     vmem = pl.BlockSpec(memory_space=pltpu.VMEM)
-    gradient, code, inverse, jac, null = local_call(
+    gradient, code, inverse, jac = local_call(
         gradient_kernel, "local_gradient",
         [
             jax.ShapeDtypeStruct(pair, jnp.float32),
             jax.ShapeDtypeStruct((blocks, LANES), jnp.int32),
             jax.ShapeDtypeStruct((blocks, PICK, LANES), jnp.int32),
             jax.ShapeDtypeStruct((blocks * PAD, LANES), jnp.float32),
-            jax.ShapeDtypeStruct(nullspace.shape, nullspace.dtype),
         ],
-        [pltpu.VMEM((blocks, LANES), jnp.int32), pltpu.SemaphoreType.DMA((blocks // CHUNK,))],
-        [vmem] * 4 + [pl.BlockSpec(memory_space=pltpu.HBM)],
-        starts, jnp.transpose(frame_ids), obs_count[None, :], residual_rows,
-        jnp.transpose(jacobian, (1, 0, 2)), nullspace,
+        [pltpu.VMEM((blocks, LANES), jnp.int32)], [vmem] * 4,
+        starts, offsets, residual_rows, jnp.transpose(jacobian, (1, 0, 2)), nullspace,
     )
     jac = jac.reshape(blocks, PAD, LANES)
 
     def product(field):
         return local_call(
             product_kernel, "local_field", [jax.ShapeDtypeStruct(pair, jnp.float32)], [], [vmem] * 5,
-            starts, field, code, inverse, jac, null,
+            starts, field, code, inverse, jac, nullspace,
         )[0]
 
     residual, direction, scale, damp = phase(

time: 101 us -> 100 us (0.990)
  local copies, waits for them, and re-layouts: 5.39 us -> 3.98 us
    unnamed x14 -> x12, local copies, waits for them, and re-layouts: 5.39 us -> 3.98 us
where the time goes in v4:
time: 100 us; the launch traced here: 99.5 us
  Pallas kernels  93.2 us (93%)
  local copies, waits for them, and re-layouts  3.98 us (4%)
  other arithmetic  1.55 us (2%)
    pallas_call x3, Pallas kernels, phase(): pl.pallas_call(functools.partial(kernel, n, m), in_specs=[vmem] * len(ope...  67.1 us
    pallas_call x3, Pallas kernels, local_call(): pl.pallas_call(kernel, in_specs=[pl.BlockSpec(memory_space=pltpu.SMEM)] +...  25.3 us
    unnamed x12, local copies, waits for them, and re-layouts  3.98 us

profile of v4, /device:TPU:0, one launch (start us, length us, event | category | flops | bytes accessed | tf_op | source)
XLA Modules:
  0.0 99.5 jit_solution(10173233342318941369)
XLA Ops:
  0.6 0.8 subtract_bitcast_fusion
  1.4 0.8 subtract_select_fusion.offs_ref
  2.2 0.0 copy-start
  2.2 2.2 %copy-done = bf16[128,128,128]{2,1,0:T(8,128)(2,1)S(1)} copy-done((bf16[128,128,128]{2,1,0:T(8,128)(2,1)S(1)}, bf16[128,128,128]{2,1,0:T(8,128)(2,1)}, u32[]{:S(2)}) %copy-start) | copy-done | bytes 4194328
  4.4 0.0 copy-start.2
  4.4 1.0 %copy-done.2 = bf16[128,15,128]{2,0,1:T(8,128)(2,1)S(1)} copy-done((bf16[128,15,128]{2,0,1:T(8,128)(2,1)S(1)}, bf16[128,15,128]{2,0,1:T(8,128)(2,1)}, u32[]{:S(2)}) %copy-start.2) | copy-done | bytes 491544
  5.4 0.0 copy-start.5
  5.4 0.8 copy-done.5
  6.2 0.0 copy-start.3
  6.2 0.0 copy-start.4
  6.2 0.0 copy-start.1
  6.2 9.2 %local_gradient.1 = (f32[64,16,128]{2,1,0:T(8,128)S(1)}, s32[128,128]{1,0:T(8,128)S(1)}, s32[128,8,128]{2,1,0:T(8,128)S(1)}, f32[2048,128]{1,0:T(8,128)S(1)}) custom-call(s32[128]{0:T(128)S(1)} %get-tuple-element.29.starts, s32[64,128]{1,0:T(8,128)S(1)} %subtract_select_fusion.offs_ref, bf16[128,128]{1,0:T(8,128)(2,1)S(1)} %copy-done.5, ...), custom_call_target="tpu_custom_call" | custom-call | tf_op jit(solution)/shard_map/local_gradient/pallas_call | solution.py:147
  15.4 0.0 copy-done.3
  15.4 0.0 copy-done.4
  15.4 21.7 %first_phase.1 = (f32[64,16,128]{2,1,0:T(8,128)S(1)}, f32[64,16,128]{2,1,0:T(8,128)S(1)}, f32[64,16,128]{2,1,0:T(8,128)S(1)}, f32[4,16,128]{2,1,0:T(8,128)S(1)}) custom-call(f32[64,16,128]{2,1,0:T(8,128)S(1)} %get-tuple-element.15.h, f32[15,4096]{1,0:T(8,128)S(1)} %copy-done.3, f32[15,4096]{1,0:T(8,128)S(1)} %copy-done.4), custom_call_target="tpu_custom_call" | custom-call | tf_op jit(solution)/shard_map/first_phase/pallas_call | solution.py:454
  37.1 0.0 copy-done.1
  37.1 8.0 %local_field.2.h = f32[64,16,128]{2,1,0:T(8,128)S(1)} custom-call(s32[128]{0:T(128)S(1)} %get-tuple-element.29.starts, f32[64,16,128]{2,1,0:T(8,128)S(1)} %get-tuple-element.16.field_ref.direction, s32[128,128]{1,0:T(8,128)S(1)} %get-tuple-element.17.code_ref, s32[128,8,128]{2,1,0:T(8,128)S(1)} %get-tuple-element.18.inv_ref, f32[128,16,128]{2,1,0:T(8,128)S(1)} %bitcast.10, ...), custom_call_target="tpu_custom_call" | custom-call | tf_op jit(solution)/shard_map/local_field/pallas_call | solution.py:147
  45.1 24.4 %middle_phase.1 = (f32[64,16,128]{2,1,0:T(8,128)S(1)}, f32[64,16,128]{2,1,0:T(8,128)S(1)}, f32[32,16,128]{2,1,0:T(8,128)S(1)}) custom-call(f32[64,16,128]{2,1,0:T(8,128)S(1)} %local_field.2.h, f32[64,16,128]{2,1,0:T(8,128)S(1)} %get-tuple-element.20.res, f32[64,16,128]{2,1,0:T(8,128)S(1)} %get-tuple-element.16.field_ref.direction, ...), custom_call_target="tpu_custom_call" | custom-call | tf_op jit(solution)/shard_map/middle_phase/pallas_call | solution.py:454
  69.5 8.0 %local_field.3.h = f32[64,16,128]{2,1,0:T(8,128)S(1)} custom-call(s32[128]{0:T(128)S(1)} %get-tuple-element.29.starts, f32[64,16,128]{2,1,0:T(8,128)S(1)} %get-tuple-element.24.field_ref.direction, s32[128,128]{1,0:T(8,128)S(1)} %get-tuple-element.17.code_ref, s32[128,8,128]{2,1,0:T(8,128)S(1)} %get-tuple-element.18.inv_ref, f32[128,16,128]{2,1,0:T(8,128)S(1)} %bitcast.11, ...), custom_call_target="tpu_custom_call" | custom-call | tf_op jit(solution)/shard_map/local_field/pallas_call | solution.py:147
  77.6 21.1 %last_phase.1 = (f32[32,16,128]{2,1,0:T(8,128)S(1)}, f32[8,128]{1,0:T(8,128)S(1)}) custom-call(f32[64,16,128]{2,1,0:T(8,128)S(1)} %local_field.3.h, f32[64,16,128]{2,1,0:T(8,128)S(1)} %get-tuple-element.23.res, f32[64,16,128]{2,1,0:T(8,128)S(1)} %get-tuple-element.24.field_ref.direction, f32[64,16,128]{2,1,0:T(8,128)S(1)} %get-tuple-element.21.scale, ...), custom_call_target="tpu_custom_call" | custom-call | tf_op jit(solution)/shard_map/last_phase/pallas_call | solution.py:454
  98.6 0.9 last_update.1
  (1 shorter events, 0.0 us)
Async XLA Ops:
  2.2 2.2 %copy-start = (bf16[128,128,128]{2,1,0:T(8,128)(2,1)S(1)}, bf16[128,128,128]{2,1,0:T(8,128)(2,1)}, u32[]{:S(2)}) copy-start(bf16[128,128,128]{2,1,0:T(8,128)(2,1)} %null_ref.5) | copy-start | bytes 12582916
  4.4 1.0 %copy-start.2 = (bf16[128,15,128]{2,0,1:T(8,128)(2,1)S(1)}, bf16[128,15,128]{2,0,1:T(8,128)(2,1)}, u32[]{:S(2)}) copy-start(bf16[128,15,128]{2,0,1:T(8,128)(2,1)} %param.8) | copy-start | bytes 1474564
  5.4 0.8 copy-start.5
  6.2 9.2 %copy-start.3 = (f32[15,4096]{1,0:T(8,128)S(1)}, f32[15,4096]{1,0:T(8,128)}, u32[]{:S(2)}) copy-start(f32[15,4096]{1,0:T(8,128)} %damping.1) | copy-start | bytes 737284
  6.2 9.2 %copy-start.4 = (f32[15,4096]{1,0:T(8,128)S(1)}, f32[15,4096]{1,0:T(8,128)}, u32[]{:S(2)}) copy-start(f32[15,4096]{1,0:T(8,128)} %jacobi_scale.1) | copy-start | bytes 737284
  6.2 30.9 %copy-start.1 = (bf16[128,128,128]{2,1,0:T(8,128)(2,1)S(1)}, bf16[128,128,128]{2,1,0:T(8,128)(2,1)}, u32[]{:S(2)}) copy-start(bf16[128,128,128]{2,1,0:T(8,128)(2,1)} %null_ref.5) | copy-start | bytes 12582916

commit v5 on v4

--- a/solution.py
+++ b/solution.py
@@ -198,17 +198,23 @@
 
     peers = [partner(i, k) for k in range(n)]
     outward = range(n - 1, 0, -1)
+    across = range(n - 2, 0, -2)
+    turns = [k + 1 for k in range(n - 2, -1, -2)] + [k for k in range(n - 2, -1, -2)]
     folds = {
         k: remote(at(h, peers[k], own), at(fold, peers[k]), fold_s.at[k], fold_r.at[k], "kf", later) for k in range(n)
     }
 
     @pl.when(w < m - 1)
     def _():
-        for k in range(n - 1, -1, -1):
+        for k in turns:
             folds[k].start()
 
     sends = []
-    for k in range(n - 1, -1, -1):
+
+    def arrived(k):
+        remote(at(acc, i), rs.at[k], rs_s.at[k], rs_r.at[k], "lm", peers[1 if k % 2 else k]).wait_recv()
+
+    for k in turns:
         spot = pl.ds(peers[k] * sh, sh)
 
         @pl.when(w > 0)
@@ -220,14 +226,17 @@
         def _():
             acc[spot] = h[spot]
 
+        if k % 2 == 0:
+            arrived(k + 1)
+            acc[spot] += rs[k + 1]
         if k > 0:
-            copy = remote(at(acc, peers[k]), rs.at[k], rs_s.at[k], rs_r.at[k], "lm", peers[k])
+            copy = remote(at(acc, peers[k]), rs.at[k], rs_s.at[k], rs_r.at[k], "lm", peers[1 if k % 2 else k])
             copy.start()
             sends.append(copy)
     here = pl.ds(i * sh, sh)
     total = acc[here]
-    for k in range(1, n):
-        remote(at(acc, i), rs.at[k], rs_s.at[k], rs_r.at[k], "lm", peers[k]).wait_recv()
+    for k in range(2, n, 2):
+        arrived(k)
         total = total + rs[k]
     value, products = on_shard(here, total)
     full[here] = value
@@ -241,7 +250,7 @@
             copy = remote(near.at[i], near.at[i], near_s.at[k], near_r.at[k], "lm", peers[k])
             copy.start()
             sends.append(copy)
-    for k in outward:
+    for k in across:
         copy = remote(at(full, i), at(full, i), ag_s.at[k], ag_r.at[k], "lm", peers[k])
         copy.start()
         sends.append(copy)
@@ -252,14 +261,23 @@
 
     def collect(k):
         if k > 0:
-            remote(at(full, peers[k]), at(full, peers[k]), ag_s.at[k], ag_r.at[k], "lm", peers[k]).wait_recv()
+            remote(
+                at(full, peers[k]), at(full, peers[k]), ag_s.at[k], ag_r.at[k], "lm", peers[1 if k % 2 else k]
+            ).wait_recv()
+        if k % 2 == 0:
+            copy = remote(
+                at(full, peers[k]), at(full, peers[k]), ag_s.at[k + 1], ag_r.at[k + 1], "lm", peers[1]
+            )
+            copy.start()
+            sends.append(copy)
         if pair:
 
             @pl.when(w > 0)
             def _():
                 forwards[k].start()
 
-    for k in range(n // 2):
+    visits = [0] + [v for k in range(2, n, 2) for v in (k, k - 1)] + [n - 1]
+    for k in visits[:n - 2]:
         collect(k)
     if products:
         for k in range(1, n):
@@ -272,7 +290,7 @@
             copy = remote(far.at[w], far.at[w], far_s.at[k], far_r.at[w], "kf", lax.rem(w + k, m))
             copy.start()
             sends.append(copy)
-    for k in range(n // 2, n):
+    for k in visits[n - 2:]:
         collect(k)
 
     def sums():

time: 100 us -> 107 us (1.070)
  Pallas kernels: 93.2 us -> 100 us
    pallas_call x3, Pallas kernels: 67.1 us -> 74.3 us  [phase(): pl.pallas_call(functools.partial(kernel, n, m), in_specs=[vmem] * len(ope...]
where the time goes in v5:
time: 107 us
  Pallas kernels  100 us (93%)
  local copies, waits for them, and re-layouts  3.98 us (4%)
  other arithmetic  1.55 us (1%)
    pallas_call x3, Pallas kernels, phase(): pl.pallas_call(functools.partial(kernel, n, m), in_specs=[vmem] * len(ope...  74.3 us
    pallas_call x3, Pallas kernels, local_call(): pl.pallas_call(kernel, in_specs=[pl.BlockSpec(memory_space=pltpu.SMEM)] +...  25.2 us
    unnamed x12, local copies, waits for them, and re-layouts  3.98 us

profile of v5, /device:TPU:0, one launch (start us, length us, event | category | flops | bytes accessed | tf_op | source)
XLA Modules:
  0.0 106.6 jit_solution(17542889813918379605)
XLA Ops:
  0.6 0.8 subtract_bitcast_fusion
  1.4 0.8 subtract_select_fusion.offs_ref
  2.2 0.0 copy-start
  2.2 2.2 %copy-done = bf16[128,128,128]{2,1,0:T(8,128)(2,1)S(1)} copy-done((bf16[128,128,128]{2,1,0:T(8,128)(2,1)S(1)}, bf16[128,128,128]{2,1,0:T(8,128)(2,1)}, u32[]{:S(2)}) %copy-start) | copy-done | bytes 4194328
  4.4 0.0 copy-start.2
  4.4 1.0 copy-done.2
  5.4 0.0 copy-start.5
  5.4 0.8 copy-done.5
  6.2 0.0 copy-start.3
  6.2 0.0 copy-start.4
  6.2 0.0 copy-start.1
  6.2 9.2 %local_gradient.1 = (f32[64,16,128]{2,1,0:T(8,128)S(1)}, s32[128,128]{1,0:T(8,128)S(1)}, s32[128,8,128]{2,1,0:T(8,128)S(1)}, f32[2048,128]{1,0:T(8,128)S(1)}) custom-call(s32[128]{0:T(128)S(1)} %get-tuple-element.29.starts, s32[64,128]{1,0:T(8,128)S(1)} %subtract_select_fusion.offs_ref, bf16[128,128]{1,0:T(8,128)(2,1)S(1)} %copy-done.5, ...), custom_call_target="tpu_custom_call" | custom-call | tf_op jit(solution)/shard_map/local_gradient/pallas_call | solution.py:147
  15.4 0.0 copy-done.3
  15.4 0.0 copy-done.4
  15.4 23.1 %first_phase.1 = (f32[64,16,128]{2,1,0:T(8,128)S(1)}, f32[64,16,128]{2,1,0:T(8,128)S(1)}, f32[64,16,128]{2,1,0:T(8,128)S(1)}, f32[4,16,128]{2,1,0:T(8,128)S(1)}) custom-call(f32[64,16,128]{2,1,0:T(8,128)S(1)} %get-tuple-element.15.h, f32[15,4096]{1,0:T(8,128)S(1)} %copy-done.3, f32[15,4096]{1,0:T(8,128)S(1)} %copy-done.4), custom_call_target="tpu_custom_call" | custom-call | tf_op jit(solution)/shard_map/first_phase/pallas_call | solution.py:472
  38.5 0.0 copy-done.1
  38.5 8.0 %local_field.2.h = f32[64,16,128]{2,1,0:T(8,128)S(1)} custom-call(s32[128]{0:T(128)S(1)} %get-tuple-element.29.starts, f32[64,16,128]{2,1,0:T(8,128)S(1)} %get-tuple-element.16.field_ref.direction, s32[128,128]{1,0:T(8,128)S(1)} %get-tuple-element.17.code_ref, s32[128,8,128]{2,1,0:T(8,128)S(1)} %get-tuple-element.18.inv_ref, f32[128,16,128]{2,1,0:T(8,128)S(1)} %bitcast.10, ...), custom_call_target="tpu_custom_call" | custom-call | tf_op jit(solution)/shard_map/local_field/pallas_call | solution.py:147
  46.5 26.9 %middle_phase.1 = (f32[64,16,128]{2,1,0:T(8,128)S(1)}, f32[64,16,128]{2,1,0:T(8,128)S(1)}, f32[32,16,128]{2,1,0:T(8,128)S(1)}) custom-call(f32[64,16,128]{2,1,0:T(8,128)S(1)} %local_field.2.h, f32[64,16,128]{2,1,0:T(8,128)S(1)} %get-tuple-element.20.res, f32[64,16,128]{2,1,0:T(8,128)S(1)} %get-tuple-element.16.field_ref.direction, ...), custom_call_target="tpu_custom_call" | custom-call | tf_op jit(solution)/shard_map/middle_phase/pallas_call | solution.py:472
  73.4 8.0 %local_field.3.h = f32[64,16,128]{2,1,0:T(8,128)S(1)} custom-call(s32[128]{0:T(128)S(1)} %get-tuple-element.29.starts, f32[64,16,128]{2,1,0:T(8,128)S(1)} %get-tuple-element.24.field_ref.direction, s32[128,128]{1,0:T(8,128)S(1)} %get-tuple-element.17.code_ref, s32[128,8,128]{2,1,0:T(8,128)S(1)} %get-tuple-element.18.inv_ref, f32[128,16,128]{2,1,0:T(8,128)S(1)} %bitcast.11, ...), custom_call_target="tpu_custom_call" | custom-call | tf_op jit(solution)/shard_map/local_field/pallas_call | solution.py:147
  81.4 24.3 %last_phase.1 = (f32[32,16,128]{2,1,0:T(8,128)S(1)}, f32[8,128]{1,0:T(8,128)S(1)}) custom-call(f32[64,16,128]{2,1,0:T(8,128)S(1)} %local_field.3.h, f32[64,16,128]{2,1,0:T(8,128)S(1)} %get-tuple-element.23.res, f32[64,16,128]{2,1,0:T(8,128)S(1)} %get-tuple-element.24.field_ref.direction, f32[64,16,128]{2,1,0:T(8,128)S(1)} %get-tuple-element.21.scale, ...), custom_call_target="tpu_custom_call" | custom-call | tf_op jit(solution)/shard_map/last_phase/pallas_call | solution.py:472
  105.7 0.9 last_update.1
  (1 shorter events, 0.0 us)
Async XLA Ops:
  2.2 2.2 %copy-start = (bf16[128,128,128]{2,1,0:T(8,128)(2,1)S(1)}, bf16[128,128,128]{2,1,0:T(8,128)(2,1)}, u32[]{:S(2)}) copy-start(bf16[128,128,128]{2,1,0:T(8,128)(2,1)} %null_ref.5) | copy-start | bytes 12582916
  4.4 1.0 copy-start.2
  5.4 0.8 copy-start.5
  6.2 9.2 %copy-start.3 = (f32[15,4096]{1,0:T(8,128)S(1)}, f32[15,4096]{1,0:T(8,128)}, u32[]{:S(2)}) copy-start(f32[15,4096]{1,0:T(8,128)} %damping.1) | copy-start | bytes 737284
  6.2 9.2 %copy-start.4 = (f32[15,4096]{1,0:T(8,128)S(1)}, f32[15,4096]{1,0:T(8,128)}, u32[]{:S(2)}) copy-start(f32[15,4096]{1,0:T(8,128)} %jacobi_scale.1) | copy-start | bytes 737284
  6.2 32.3 %copy-start.1 = (bf16[128,128,128]{2,1,0:T(8,128)(2,1)S(1)}, bf16[128,128,128]{2,1,0:T(8,128)(2,1)}, u32[]{:S(2)}) copy-start(bf16[128,128,128]{2,1,0:T(8,128)(2,1)} %null_ref.5) | copy-start | bytes 12582916
